TPU v7x, 128 devices: a whole 4x4x4 slice. The times are simulated.
128 devices in a mesh: tm: 4 (over y), space: 32 (over x, z, core).
Axes of the slice: x: 4, y: 4, z: 4, core: 2. Of those that a mesh axis runs over, the one named last changes fastest.
Arguments:
- vectors: bfloat16 [8, 2, 3, 16384, 384], P('tm', None, None, 'space'), may hold values from -6 to 6
- perambulators: bfloat16 [128, 2, 384, 384], P(('tm', 'space')), may hold values from -0.0007324219 to 0.0007324219
- item_block: int32 [128, 128], P(('tm', 'space')), may hold values from 0 to 3
- item_owner: int32 [128, 128], P(('tm', 'space')), may hold values from 0 to 127, as said below
- momenta: int32 [2, 3], replicated, may hold values from -2 to 2, as said below
Outputs:
- contracted: bfloat16 [128, 128, 2, 12, 768], P(('tm', 'space'))
Inputs may be any that keep to these rules, and one draw needn't show every extreme that they name: `item_owner`: in every device's list no owner appears more than 2 times, and some owners appear exactly 2 times in the lists of all devices. `momenta`: the first component of every momentum is nonzero.
All inputs are finite; a program needn't handle non-finite values.
Results may differ from a plain program's by a relative error of at most 0.0057.
Values may be sent and summed in bfloat16 or wider, within the bound.
A program may use at most 128 MiB of HBM per device.

v0:
```python
import math

import jax
import jax.numpy as jnp
from jax import lax
from jax.sharding import Mesh
from jax.sharding import PartitionSpec as P

LX = 64
CAP = 2
SPACE = ("space_0", "space_1", "space_2")
TM_SPACE = ("tm", "space_0", "space_1", "space_2")


def split_up(x, dim, size):
    shape = x.shape
    pieces = x.reshape(*shape[:dim], size, shape[dim] // size, *shape[dim + 1 :])
    return jnp.moveaxis(pieces, dim, 0)


def sum_at_owner(x, axis, dim):
    pieces = split_up(x, dim, lax.axis_size(axis))
    arrived = lax.all_to_all(pieces, axis, split_axis=0, concat_axis=0, tiled=True)
    return arrived.sum(axis=0)


def sum_in_two_steps(x, axes, dim):
    far, near = axes
    own = sum_at_owner(split_up(x, dim, lax.axis_size(far)), near, dim + 1)
    return jnp.sum(lax.all_to_all(own, far, 0, 0, tiled=True), axis=0)


def site_phase(momenta, first_site, site_count):
    site_index = first_site + jnp.arange(site_count, dtype=jnp.int32)
    coord_x = site_index % LX
    coord_y = site_index // LX % LX
    coord_z = site_index // (LX * LX)
    phase_turns = (
        momenta[:, 0:1] * coord_x[None, :]
        + momenta[:, 1:2] * coord_y[None, :]
        + momenta[:, 2:3] * coord_z[None, :]
    ) % LX
    phase_angle = phase_turns.astype(jnp.float32) * (2.0 * math.pi / LX)
    return (jnp.cos(phase_angle), jnp.sin(phase_angle))


def twisted_right(vectors, cosines, sines):
    real_part = vectors[:, 0].astype(jnp.float32)[:, None]
    imag_part = vectors[:, 1].astype(jnp.float32)[:, None]
    cosine = cosines[None, :, None, :, None]
    sine_term = sines[None, :, None, :, None]
    twisted_real = (cosine * real_part + sine_term * imag_part).astype(jnp.bfloat16)
    twisted_imag = (cosine * imag_part - sine_term * real_part).astype(jnp.bfloat16)
    upper_half = jnp.stack([twisted_real, twisted_imag], axis=2)
    lower_half = jnp.stack([twisted_imag, -twisted_real], axis=2)
    shape_lead = upper_half.shape
    inner_rows = shape_lead[2] * shape_lead[3] * shape_lead[4]
    return jnp.concatenate(
        [
            upper_half.reshape(shape_lead[0], shape_lead[1], inner_rows, shape_lead[5]),
            lower_half.reshape(shape_lead[0], shape_lead[1], inner_rows, shape_lead[5]),
        ],
        axis=-1,
    )


def slot_table(block_ids, owners, devices, pad_block):
    item_count = owners.shape[0]
    position_list = jnp.arange(item_count, dtype=jnp.int32)
    earlier = (owners[None, :] == owners[:, None]) & (
        position_list[None, :] < position_list[:, None]
    )
    slot_rank = jnp.sum(earlier.astype(jnp.int32), axis=1)
    target = owners * CAP + slot_rank
    return jnp.full((devices * CAP,), pad_block, jnp.int32).at[target].set(block_ids)


def complex_kernel(pair):
    top_rows = jnp.concatenate([pair[0], pair[1]], axis=1)
    bottom_rows = jnp.concatenate([-pair[1], pair[0]], axis=1)
    return jnp.concatenate([top_rows, bottom_rows], axis=0)


def body(vectors, perambulators, item_block, item_owner, momenta):
    group_count = lax.axis_size("tm")
    space_count = lax.axis_size(SPACE)
    devices = group_count * space_count
    slab_count = vectors.shape[0]
    site_count = vectors.shape[3]
    vector_width = vectors.shape[4]
    first_site = lax.axis_index(SPACE) * site_count
    cosines, sines = site_phase(momenta, first_site, site_count)
    right_side = twisted_right(vectors, cosines, sines)
    left_side = vectors.reshape(slab_count, -1, vector_width)
    partial_value = jnp.einsum(
        "tmk,tpmj->tpkj", left_side, right_side, preferred_element_type=jnp.float32
    )
    block_rows = sum_in_two_steps(partial_value, (("space_0", "space_1"), "space_2"), 2)
    row_block = block_rows.shape[2]
    full_width = block_rows.shape[3]
    blocks = block_rows.astype(jnp.bfloat16).reshape(-1, row_block, full_width)
    block_total = blocks.shape[0]
    padded = jnp.concatenate([blocks, jnp.zeros((1, row_block, full_width), jnp.bfloat16)], axis=0)
    table = slot_table(item_block[0], item_owner[0], devices, block_total)
    outgoing = jnp.take(padded, table, axis=0).reshape(devices, CAP, row_block, full_width)
    kernel = complex_kernel(perambulators[0])
    received = lax.all_to_all(outgoing, TM_SPACE, split_axis=0, concat_axis=0, tiled=True)
    product = jnp.dot(received.reshape(-1, full_width), kernel, preferred_element_type=jnp.float32)
    result = product.astype(jnp.bfloat16).reshape(received.shape)
    return result[None]


def solution(mesh):
    split = Mesh(
        mesh.devices.reshape(mesh.shape["tm"], 4, 4, 2), ("tm", "space_0", "space_1", "space_2")
    )
    in_specs = (
        P("tm", None, None, SPACE, None),
        P(TM_SPACE, None, None, None),
        P(TM_SPACE, None),
        P(TM_SPACE, None),
        P(),
    )
    out_specs = P(TM_SPACE, None, None, None, None)
    return jax.shard_map(body, mesh=split, in_specs=in_specs, out_specs=out_specs, check_vma=False)
```

profile of v0, /device:TPU:1, one launch (start us, length us, event | category | flops | bytes accessed | tf_op | source)
XLA Modules:
  0.0 224.0 jit_solution(13541465781880526389)
XLA Ops:
  0.0 1.0 slice_reduce_fusion.2
  1.0 0.2 fusion.27
  1.2 0.1 sin.7
  1.3 3.3 %bitcast_convert_fusion.1 = (f32[2,3,512,384]{3,2,1,0:T(8,128)S(1)}, f32[2,3,512,384]{3,2,1,0:T(8,128)S(1)}) fusion(bf16[2,2,3,512,384]{4,3,2,1,0:T(8,128)(2,1)} %param.5), kind=kLoop, calls=%fused_computation.13 | loop fusion | flops 2359296 | bytes 14155776 | tf_op jit(solution)/shard_map/mul | solution.py:52
  4.6 2.1 fusion.26
  6.6 1.4 subtract_convert_fusion
  8.1 7.4 %pad_maximum_fusion = (bf16[2,2,2,3,512,384]{5,4,3,2,1,0:T(8,128)(2,1)}, bf16[2,2,2,3,512,384]{5,4,3,2,1,0:T(8,128)(2,1)}) fusion(bf16[2,2,1,3,512,384]{5,4,3,2,1,0:T(8,128)(2,1)S(1)} %subtract_convert_fusion, bf16[2,2,1,3,512,384]{5,4,3,2,1,0:T(8,128)(2,1)S(1)} %get-tuple-element.9, bf16[2,2,1,3,512,384]{5,4,3,2,1,0:T(8,128)(2,1)S(1)} %get-tuple-element.8), kind=kLoop, calls=%fused_computation.6 | loop fusion | flops 9437184 | bytes 33030144 | tf_op jit(solution)/shard_map/stack | solution.py:54
  15.5 13.6 %fusion = f32[2,2,768,384]{2,3,1,0:T(8,128)} fusion(bf16[2,3072,384,1]{2,1,3,0:T(8,128)(2,1)} %bitcast.45, bf16[2,2,3072,384]{3,2,1,0:T(8,128)(2,1)} %bitcast.44, bf16[2,2,3072,384]{3,2,1,0:T(8,128)(2,1)} %bitcast.43), kind=kOutput, calls=%fused_computation.2 | convolution fusion | flops 7285506048 | bytes 28311552 | tf_op jit(solution)/shard_map/tmk,tpmj->tpkj/dot_general | solution.py:95
  29.1 3.8 %copy.46 = f32[2,2,16,24,768]{4,2,3,1,0:T(8,128)S(1)} copy(f32[2,2,16,24,768]{4,3,2,1,0:T(8,128)} %bitcast.46) | data formatting | bytes 9437184 | tf_op jit(solution)/shard_map/reshape | solution.py:17
  32.9 0.3 copy.47
  33.2 9.7 %all_to_all.15 = f32[2,16,2,2,12,768]{5,1,4,3,2,0:T(8,128)} all-to-all(f32[2,16,2,2,12,768]{5,1,4,3,2,0:T(8,128)S(1)} %copy.47), channel_id=1, replica_groups=mesh['tm'=4,'space_0'=4,'space_1'=4,'space_2'=2] {'space_2'}, dimensions={0} | all-to-all | bytes 9437184 | tf_op jit(solution)/shard_map/all_to_all | solution.py:23
  42.9 3.0 %reduce_sum.31 = f32[16,2,2,12,768]{4,0,3,2,1:T(8,128)S(1)} reduce(f32[2,16,2,2,12,768]{5,1,4,3,2,0:T(8,128)} %all_to_all.15, f32[]{:T(128)} %constant.93.clone.1), dimensions={0}, to_apply=%region_2.3 | reduce | flops 589824 | bytes 7077892 | tf_op jit(solution)/shard_map/reduce_sum | solution.py:24
  45.9 0.0 copy-start.1
  45.9 3.2 %copy.49 = f32[16,2,2,12,768]{4,2,3,1,0:T(2,128)} copy(f32[16,2,2,12,768]{4,0,3,2,1:T(8,128)S(1)} %reduce_sum.31) | data formatting | bytes 4718592 | tf_op jit(solution)/shard_map/reduce_sum | solution.py:24
  49.1 7.7 %all-to-all-start.1 = ((f32[16,2,2,12,768]{4,2,3,1,0:T(2,128)}), f32[16,2,2,12,768]{4,2,3,1,0:T(2,128)S(1)}, u32[]{:S(2)}, u32[]{:S(2)}) async-start(f32[16,2,2,12,768]{4,2,3,1,0:T(2,128)} %copy.49), calls=%async_computation.1 | async-start | bytes 4718592 | tf_op jit(solution)/shard_map/all_to_all | solution.py:30
  56.8 0.2 convert_reduce_fusion
  57.0 1.1 scatter_custom_fusion
  58.1 0.2 broadcast_in_dim.14
  58.3 30.4 %all-to-all-done.1 = f32[16,2,2,12,768]{4,2,3,1,0:T(2,128)S(1)} async-done(((f32[16,2,2,12,768]{4,2,3,1,0:T(2,128)}), f32[16,2,2,12,768]{4,2,3,1,0:T(2,128)S(1)}, u32[]{:S(2)}, u32[]{:S(2)}) %all-to-all-start.1) | async-done | bytes 2359328 | tf_op jit(solution)/shard_map/all_to_all | solution.py:30
  88.7 0.9 reduce_sum.32
  89.7 3.6 %gather_fusion = bf16[256,12,768]{2,1,0:T(8,128)(2,1)} fusion(bf16[5,12,768]{2,1,0:T(8,128)(2,1)S(1)} %concatenate.16, s32[1024]{0:T(1024)S(1)} %pad_clamp_fusion), kind=kCustom, calls=%fused_computation | custom fusion | bytes 9438208 | tf_op jit(solution)/shard_map/jit(_take)/gather | solution.py:105
  93.3 11.0 %broadcast_select_fusion = bf16[128,2,12,768]{3,1,0,2:T(2,128)(2,1)} fusion(pred[128,2]{1,0:T(8,128)(4,1)S(1)} %broadcast_in_dim.14, bf16[128,2,12,768]{3,2,1,0:T(8,128)(2,1)} %bitcast.41), kind=kLoop, calls=%fused_computation.10 | loop fusion | flops 2359296 | bytes 9437440 | tf_op jit(solution)/shard_map/jit(_take)/select_n | solution.py:105
  104.3 7.7 %copy.52 = bf16[128,2,12,768]{3,1,2,0:T(2,128)(2,1)} copy(bf16[128,2,12,768]{3,1,0,2:T(2,128)(2,1)} %broadcast_select_fusion) | data formatting | bytes 9437184 | tf_op jit(solution)/shard_map/jit(_take)/select_n | solution.py:105
  112.0 10.1 %all-to-all-start.2 = ((bf16[128,2,12,768]{3,1,2,0:T(2,128)(2,1)}), bf16[128,2,12,768]{3,1,2,0:T(2,128)(2,1)}, u32[]{:S(2)}, u32[]{:S(2)}) async-start(bf16[128,2,12,768]{3,1,2,0:T(2,128)(2,1)} %copy.52), calls=%async_computation.2 | async-start | bytes 9437184 | tf_op jit(solution)/shard_map/all_to_all | solution.py:107
  122.1 0.0 copy-done
  122.1 0.1 slice_bitcast_fusion
  122.2 58.2 %all-to-all-done.2 = bf16[128,2,12,768]{3,1,2,0:T(2,128)(2,1)} async-done(((bf16[128,2,12,768]{3,1,2,0:T(2,128)(2,1)}), bf16[128,2,12,768]{3,1,2,0:T(2,128)(2,1)}, u32[]{:S(2)}, u32[]{:S(2)}) %all-to-all-start.2) | async-done | bytes 4718624 | tf_op jit(solution)/shard_map/all_to_all | solution.py:107
  180.4 6.4 %copy.53 = bf16[128,2,12,768]{3,2,1,0:T(8,128)(2,1)} copy(bf16[128,2,12,768]{3,1,2,0:T(2,128)(2,1)} %all-to-all-done.2) | data formatting | bytes 9437184 | tf_op jit(solution)/shard_map/all_to_all | solution.py:107
  186.8 8.3 %reshape.344 = bf16[3072,768]{1,0:T(8,128)(2,1)} reshape(bf16[128,2,12,768]{3,2,1,0:T(8,128)(2,1)} %copy.53) | data formatting | bytes 9437184 | tf_op jit(solution)/shard_map/reshape | solution.py:108
  195.2 11.9 %convolution_convert_fusion = bf16[3072,768]{1,0:T(8,128)(2,1)} fusion(bf16[3072,768]{1,0:T(8,128)(2,1)} %reshape.344, bf16[384,384]{1,0:T(8,128)(2,1)S(1)} %get-tuple-element.17, bf16[384,384]{1,0:T(8,128)(2,1)S(1)} %fusion.25, bf16[384,384]{1,0:T(8,128)(2,1)S(1)} %get-tuple-element.16), kind=kOutput, calls=%fused_computation.11 | convolution fusion | flops 3630956544 | bytes 10321920 | tf_op jit(solution)/shard_map/dot_general | solution.py:108
  207.1 8.3 %broadcast_in_dim_reshape.3 = bf16[1,128,2,12,768]{4,3,2,1,0:T(8,128)(2,1)} reshape(bf16[3072,768]{1,0:T(8,128)(2,1)} %convolution_convert_fusion) | data formatting | bytes 9437184 | tf_op jit(solution)/shard_map/broadcast_in_dim;reshape | solution.py:110
  215.4 8.6 %copy.54 = bf16[1,128,2,12,768]{4,2,3,1,0:T(2,128)(2,1)} copy(bf16[1,128,2,12,768]{4,3,2,1,0:T(8,128)(2,1)} %broadcast_in_dim_reshape.3) | data formatting | bytes 9437184 | tf_op jit(solution)/shard_map/broadcast_in_dim;reshape | solution.py:110
  (11 shorter events, 0.1 us)
Async XLA Ops:
  45.9 10.9 %copy-start.1 = (s32[1,128]{1,0:T(1,128)S(1)}, s32[1,128]{1,0:T(1,128)}, u32[]{:S(2)}) copy-start(s32[1,128]{1,0:T(1,128)} %param.8) | copy-start | bytes 1540
  49.1 39.6 %all-to-all-start.1 = ((f32[16,2,2,12,768]{4,2,3,1,0:T(2,128)}), f32[16,2,2,12,768]{4,2,3,1,0:T(2,128)S(1)}, u32[]{:S(2)}, u32[]{:S(2)}) async-start(f32[16,2,2,12,768]{4,2,3,1,0:T(2,128)} %copy.49), calls=%async_computation.1 | async-start | bytes 4718592 | tf_op jit(solution)/shard_map/all_to_all | solution.py:30
  112.0 10.1 %copy-start = (bf16[1,2,384,384]{3,2,1,0:T(8,128)(2,1)S(1)}, bf16[1,2,384,384]{3,2,1,0:T(8,128)(2,1)}, u32[]{:S(2)}) copy-start(bf16[1,2,384,384]{3,2,1,0:T(8,128)(2,1)} %param.6) | copy-start | bytes 1769476
  112.0 68.4 %all-to-all-start.2 = ((bf16[128,2,12,768]{3,1,2,0:T(2,128)(2,1)}), bf16[128,2,12,768]{3,1,2,0:T(2,128)(2,1)}, u32[]{:S(2)}, u32[]{:S(2)}) async-start(bf16[128,2,12,768]{3,1,2,0:T(2,128)(2,1)} %copy.52), calls=%async_computation.2 | async-start | bytes 9437184 | tf_op jit(solution)/shard_map/all_to_all | solution.py:107
where the time goes:
time: 225 us; the launch traced here: 224 us
  waiting for transfers between devices  88.6 us (39%)
  local copies, waits for them, and re-layouts  52.7 us (23%)
  other arithmetic  29.5 us (13%)
  matrix products  25.5 us (11%)
  starting transfers between devices  17.8 us (8%)
  blocking collectives  9.66 us (4%)
    all_to_all x1, waiting for transfers between devices, body(): lax.all_to_all(outgoing, TM_SPACE, split_axis=0, concat_axis=0, tiled=True)  58.2 us
    all_to_all x1, waiting for transfers between devices, sum_in_two_steps(): return jnp.sum(lax.all_to_all(own, far, 0, 0, tiled=True), axis=0)  30.4 us
    another operation x2, local copies, waits for them, and re-layouts, body(): return result[None]  16.9 us
    dot_general x1, matrix products, body(): jnp.einsum('tmk,tpmj->tpkj', left_side, right_side, preferred_element_typ...  13.6 us
    dot_general x1, matrix products, body(): jnp.dot(received.reshape(-1, full_width), kernel, preferred_element_type=...  11.9 us
    select_n x2, other arithmetic, body(): jnp.take(padded, table, axis=0).reshape(devices, CAP, row_block, full_width)  11 us
    all_to_all x1, starting transfers between devices, body(): lax.all_to_all(outgoing, TM_SPACE, split_axis=0, concat_axis=0, tiled=True)  10.1 us
    all_to_all x1, blocking collectives, sum_at_owner(): lax.all_to_all(pieces, axis, split_axis=0, concat_axis=0, tiled=True)  9.66 us
  transfers between devices with their start and end apart: 2, of which 2 were waited for; matrix products, arithmetic and copies ran while one was open for 1% of the time, Pallas kernels for 0%

commit v1 on v0

--- a/solution.py
+++ b/solution.py
@@ -10,24 +10,6 @@
 CAP = 2
 SPACE = ("space_0", "space_1", "space_2")
 TM_SPACE = ("tm", "space_0", "space_1", "space_2")
-
-
-def split_up(x, dim, size):
-    shape = x.shape
-    pieces = x.reshape(*shape[:dim], size, shape[dim] // size, *shape[dim + 1 :])
-    return jnp.moveaxis(pieces, dim, 0)
-
-
-def sum_at_owner(x, axis, dim):
-    pieces = split_up(x, dim, lax.axis_size(axis))
-    arrived = lax.all_to_all(pieces, axis, split_axis=0, concat_axis=0, tiled=True)
-    return arrived.sum(axis=0)
-
-
-def sum_in_two_steps(x, axes, dim):
-    far, near = axes
-    own = sum_at_owner(split_up(x, dim, lax.axis_size(far)), near, dim + 1)
-    return jnp.sum(lax.all_to_all(own, far, 0, 0, tiled=True), axis=0)
 
 
 def site_phase(momenta, first_site, site_count):
@@ -64,15 +46,16 @@
     )
 
 
-def slot_table(block_ids, owners, devices, pad_block):
-    item_count = owners.shape[0]
-    position_list = jnp.arange(item_count, dtype=jnp.int32)
-    earlier = (owners[None, :] == owners[:, None]) & (
-        position_list[None, :] < position_list[:, None]
-    )
-    slot_rank = jnp.sum(earlier.astype(jnp.int32), axis=1)
-    target = owners * CAP + slot_rank
-    return jnp.full((devices * CAP,), pad_block, jnp.int32).at[target].set(block_ids)
+def slot_ids(lists, me, pad_block):
+    mine = lists[:, 1, :] == me
+    item_count = lists.shape[2]
+    upper = jnp.triu(jnp.ones((item_count, item_count), jnp.bfloat16))
+    rank = jnp.dot(mine.astype(jnp.bfloat16), upper, preferred_element_type=jnp.float32)
+    shifted = lists[:, 0, :] - pad_block
+    picks = [
+        jnp.sum(jnp.where(mine & (rank == float(s + 1)), shifted, 0), axis=1) for s in range(CAP)
+    ]
+    return jnp.stack(picks, axis=1) + pad_block
 
 
 def complex_kernel(pair):
@@ -95,18 +78,22 @@
     partial_value = jnp.einsum(
         "tmk,tpmj->tpkj", left_side, right_side, preferred_element_type=jnp.float32
     )
-    block_rows = sum_in_two_steps(partial_value, (("space_0", "space_1"), "space_2"), 2)
-    row_block = block_rows.shape[2]
-    full_width = block_rows.shape[3]
-    blocks = block_rows.astype(jnp.bfloat16).reshape(-1, row_block, full_width)
-    block_total = blocks.shape[0]
-    padded = jnp.concatenate([blocks, jnp.zeros((1, row_block, full_width), jnp.bfloat16)], axis=0)
-    table = slot_table(item_block[0], item_owner[0], devices, block_total)
-    outgoing = jnp.take(padded, table, axis=0).reshape(devices, CAP, row_block, full_width)
+    row_block = vector_width // space_count
+    full_width = partial_value.shape[3]
+    block_total = slab_count * momenta.shape[0]
+    flat = partial_value.astype(jnp.bfloat16).reshape(-1, full_width)
+    blocks = lax.psum_scatter(flat, SPACE, scatter_dimension=0, tiled=True)
+    lists = lax.all_gather(jnp.concatenate([item_block, item_owner], axis=0), TM_SPACE)
+    ids = slot_ids(lists, lax.axis_index(TM_SPACE), block_total)
+    everyone = lax.all_gather(blocks, TM_SPACE, tiled=True).reshape(-1, row_block, full_width)
+    padded = jnp.concatenate([everyone, jnp.zeros((1, row_block, full_width), jnp.bfloat16)], axis=0)
+    device = jnp.arange(devices)[:, None]
+    place = (device // space_count * block_total + ids) * space_count + device % space_count
+    rows = jnp.where(ids < block_total, place, devices * block_total)
+    received = jnp.take(padded, rows.reshape(-1), axis=0)
     kernel = complex_kernel(perambulators[0])
-    received = lax.all_to_all(outgoing, TM_SPACE, split_axis=0, concat_axis=0, tiled=True)
     product = jnp.dot(received.reshape(-1, full_width), kernel, preferred_element_type=jnp.float32)
-    result = product.astype(jnp.bfloat16).reshape(received.shape)
+    result = product.astype(jnp.bfloat16).reshape(devices, CAP, row_block, full_width)
     return result[None]
 
 

time: 225 us -> 269 us (1.20)
  waiting for transfers between devices: 88.6 us -> 118 us
  blocking collectives: 9.66 us -> 37.4 us
  starting transfers between devices: 17.8 us -> 0.04 us
  other arithmetic: 29.5 us -> 14.6 us
  between operations: 0.18 us -> 13.6 us
  local copies, waits for them, and re-layouts: 52.7 us -> 61.9 us
  matrix products: 25.5 us -> 22.1 us
    all_to_all x2 -> x0, waiting for transfers between devices: 88.6 us -> none  [the longest x1 58.2 us: body(): lax.all_to_all(outgoing, TM_SPACE, split_axis=0, concat_axis=0, tiled=True)]
    reduce_scatter x0 -> x1, waiting for transfers between devices: none -> 81.1 us  [body(): blocks = lax.psum_scatter(flat, SPACE, scatter_dimension=0, tiled=True)]
    all_gather x0 -> x1, blocking collectives: none -> 37.4 us  [body(): lax.all_gather(jnp.concatenate([item_block, item_owner], axis=0), TM_SPACE)]
    all_gather x0 -> x1, waiting for transfers between devices: none -> 36.7 us  [body(): lax.all_gather(blocks, TM_SPACE, tiled=True)]
    all_to_all x2 -> x0, starting transfers between devices: 17.8 us -> none  [the longest x1 10.1 us: body(): lax.all_to_all(outgoing, TM_SPACE, split_axis=0, concat_axis=0, tiled=True)]
    gather x1 -> x2, local copies, waits for them, and re-layouts: 3.62 us -> 16.5 us  [body(): received = jnp.take(padded, rows.reshape(-1), axis=0)]
    concatenate x1, local copies, waits for them, and re-layouts: 0.01 us -> 11.2 us  [body(): jnp.concatenate([everyone, jnp.zeros((1, row_block, full_width), jnp.bflo...]
    select_n x3, other arithmetic: 11 us -> 0.02 us  [the longest x1 0.02 us: body(): rows = jnp.where(ids < block_total, place, devices * block_total)]
where the time goes in v1:
time: 269 us; the launch traced here: 267 us
  waiting for transfers between devices  118 us (44%)
  local copies, waits for them, and re-layouts  61.9 us (23%)
  blocking collectives  37.4 us (14%)
  matrix products  22.1 us (8%)
  other arithmetic  14.6 us (5%)
  between operations  13.6 us (5%)
    reduce_scatter x1, waiting for transfers between devices, body(): blocks = lax.psum_scatter(flat, SPACE, scatter_dimension=0, tiled=True)  81.1 us
    all_gather x1, blocking collectives, body(): lax.all_gather(jnp.concatenate([item_block, item_owner], axis=0), TM_SPACE)  37.4 us
    all_gather x1, waiting for transfers between devices, body(): lax.all_gather(blocks, TM_SPACE, tiled=True)  36.7 us
    another operation x2, local copies, waits for them, and re-layouts, body(): return result[None]  16.9 us
    gather x2, local copies, waits for them, and re-layouts, body(): received = jnp.take(padded, rows.reshape(-1), axis=0)  16.5 us
    reshape x1, local copies, waits for them, and re-layouts, body(): lax.all_gather(blocks, TM_SPACE, tiled=True)  15.3 us
    dot_general x1, matrix products, body(): jnp.einsum('tmk,tpmj->tpkj', left_side, right_side, preferred_element_typ...  13.3 us
    concatenate x1, local copies, waits for them, and re-layouts, body(): jnp.concatenate([everyone, jnp.zeros((1, row_block, full_width), jnp.bflo...  11.2 us
  transfers between devices with their start and end apart: 2, of which 2 were waited for; matrix products, arithmetic and copies ran while one was open for 1% of the time, Pallas kernels for 0%

profile of v1, /device:TPU:1, one launch (start us, length us, event | category | flops | bytes accessed | tf_op | source)
XLA Modules:
  0.0 267.5 jit_solution(16349529939203434647)
XLA Ops:
  6.5 0.0 reduce-scatter.2.cloned.1.call-start
  6.6 1.0 slice_reduce_fusion.2
  7.6 0.2 fusion.42
  7.7 0.1 sin.7
  7.8 3.3 %bitcast_convert_fusion.1 = (f32[2,3,512,384]{3,2,1,0:T(8,128)S(1)}, f32[2,3,512,384]{3,2,1,0:T(8,128)S(1)}) fusion(bf16[2,2,3,512,384]{4,3,2,1,0:T(8,128)(2,1)} %param.5), kind=kLoop, calls=%fused_computation.13 | loop fusion | flops 2359296 | bytes 14155776 | tf_op jit(solution)/shard_map/mul | solution.py:34
  11.1 2.1 fusion.41
  13.2 1.4 subtract_convert_fusion
  14.6 7.5 %pad_maximum_fusion = (bf16[2,2,2,3,512,384]{5,4,3,2,1,0:T(8,128)(2,1)}, bf16[2,2,2,3,512,384]{5,4,3,2,1,0:T(8,128)(2,1)}) fusion(bf16[2,2,1,3,512,384]{5,4,3,2,1,0:T(8,128)(2,1)S(1)} %subtract_convert_fusion, bf16[2,2,1,3,512,384]{5,4,3,2,1,0:T(8,128)(2,1)S(1)} %get-tuple-element.11, bf16[2,2,1,3,512,384]{5,4,3,2,1,0:T(8,128)(2,1)S(1)} %get-tuple-element.10), kind=kLoop, calls=%fused_computation.5 | loop fusion | flops 9437184 | bytes 33030144 | tf_op jit(solution)/shard_map/stack | solution.py:36
  22.1 13.3 %fusion.7 = bf16[2,2,768,384]{2,3,1,0:T(8,128)(2,1)} fusion(bf16[2,3072,384,1]{2,1,3,0:T(8,128)(2,1)} %bitcast.48, bf16[2,2,3072,384]{3,2,1,0:T(8,128)(2,1)} %bitcast.47, bf16[2,2,3072,384]{3,2,1,0:T(8,128)(2,1)} %bitcast.46), kind=kOutput, calls=%fused_computation.15 | convolution fusion | flops 7286685696 | bytes 25952256 | tf_op jit(solution)/shard_map/tmk,tpmj->tpkj/dot_general | solution.py:78
  35.4 0.0 reduce-scatter.2.cloned.1.call-update
  35.4 0.0 all-gather.4.cloned.1.call-start
  35.5 81.1 %reduce-scatter.2.cloned.1.call-done = bf16[48,768]{1,0:T(8,128)(2,1)} async-done(((bf16[1536,768]{1,0:T(8,128)(2,1)}), bf16[48,768]{1,0:T(8,128)(2,1)}) %reduce-scatter.2.cloned.1.call-update) | async-done | bytes 73744 | tf_op jit(solution)/shard_map/reduce_scatter | solution.py:85
  116.6 0.0 all-gather.4.cloned.1.call-update
  116.7 37.4 %all-gather.1 = s32[128,2,128]{2,1,0:T(2,128)S(1)} all-gather(s32[1,2,128]{2,1,0:T(2,128)S(1)} %add_bitcast_fusion), channel_id=2, replica_groups=mesh['tm'=4,'space_0'=4,'space_1'=4,'space_2'=2] {'tm','space_0','space_..., dimensions={0}, use_global_device_ids=true | all-gather | bytes 132096 | tf_op jit(solution)/shard_map/all_gather | solution.py:86
  154.1 0.1 fusion.44
  154.2 0.1 copy.22
  154.3 0.1 copy.23
  154.4 0.3 fusion.17
  154.7 0.1 copy.15
  154.8 0.1 reshape.444
  155.0 0.1 reshape.440
  155.1 0.1 broadcast_in_dim.45
  155.2 0.1 broadcast_in_dim.46
  155.5 0.1 slice_bitcast_fusion
  155.5 36.7 %all-gather.4.cloned.1.call-done = bf16[6144,768]{1,0:T(8,128)(2,1)} async-done(((bf16[48,768]{1,0:T(8,128)(2,1)}), bf16[6144,768]{1,0:T(8,128)(2,1)}) %all-gather.4.cloned.1.call-update) | async-done | bytes 9437200 | tf_op jit(solution)/shard_map/all_gather | solution.py:88
  192.3 15.3 %reshape.438 = bf16[512,12,768]{2,1,0:T(8,128)(2,1)} reshape(bf16[6144,768]{1,0:T(8,128)(2,1)} %all-gather.4.cloned.1.call-done) | data formatting | bytes 18874368 | tf_op jit(solution)/shard_map/reshape | solution.py:88
  207.6 11.2 %concatenate.20 = bf16[513,12,768]{2,1,0:T(8,128)(2,1)} pad(bf16[512,12,768]{2,1,0:T(8,128)(2,1)} %reshape.438, bf16[]{:T(256)} %constant.118.clone.1), padding=0_1x0_0x0_0 | pad | bytes 18892802 | tf_op jit(solution)/shard_map/concatenate | solution.py:89
  218.8 8.1 %gather_fusion = bf16[256,12,768]{2,1,0:T(8,128)(2,1)} fusion(bf16[513,12,768]{2,1,0:T(8,128)(2,1)} %concatenate.20, s32[1024]{0:T(1024)S(1)} %pad_clamp_fusion), kind=kCustom, calls=%fused_computation | custom fusion | bytes 9438208 | tf_op jit(solution)/shard_map/jit(_take)/gather | solution.py:93
  226.9 8.3 %gather.7 = bf16[3072,768]{1,0:T(8,128)(2,1)} reshape(bf16[256,12,768]{2,1,0:T(8,128)(2,1)} %gather_fusion) | data formatting | bytes 9437184 | tf_op jit(solution)/shard_map/jit(_take)/gather | solution.py:93
  235.2 8.5 %convolution_convert_fusion = bf16[3072,768]{1,0:T(8,128)(2,1)} fusion(bf16[3072,768]{1,0:T(8,128)(2,1)} %gather.7, pred[3072]{0:T(1024)(128)(4,1)S(1)} %broadcast_in_dim.46, bf16[384,384]{1,0:T(8,128)(2,1)S(1)} %get-tuple-element.19, bf16[384,384]{1,0:T(8,128)(2,1)S(1)} %fusion.40, bf16[384,384]{1,0:T(8,128)(2,1)S(1)} %get-tuple-element.18), kind=kOutput, calls=%fused_computation.9 | convolution fusion | flops 3633315840 | bytes 10324992 | tf_op jit(solution)/shard_map/dot_general | solution.py:95
  243.8 8.3 %broadcast_in_dim_reshape.3 = bf16[1,128,2,12,768]{4,3,2,1,0:T(8,128)(2,1)} reshape(bf16[3072,768]{1,0:T(8,128)(2,1)} %convolution_convert_fusion) | data formatting | bytes 9437184 | tf_op jit(solution)/shard_map/broadcast_in_dim;reshape | solution.py:97
  252.0 8.6 %copy.18 = bf16[1,128,2,12,768]{4,2,3,1,0:T(2,128)(2,1)} copy(bf16[1,128,2,12,768]{4,3,2,1,0:T(8,128)(2,1)} %broadcast_in_dim_reshape.3) | data formatting | bytes 9437184 | tf_op jit(solution)/shard_map/broadcast_in_dim;reshape | solution.py:97
  (16 shorter events, 0.1 us)
Async XLA Ops:
  6.5 110.1 %reduce-scatter.2.cloned.1.call-start = ((), (), s32[]{:S(2)}) async-start(), calls=%async_computation.1 | async-start | bytes 2433024 | tf_op jit(solution)/shard_map/reduce_scatter | solution.py:85
  22.1 94.5 %copy-start.1 = (s32[1,128]{1,0:T(1,128)S(1)}, s32[1,128]{1,0:T(1,128)}, u32[]{:S(2)}) copy-start(s32[1,128]{1,0:T(1,128)} %param.8) | copy-start | bytes 1540
  22.1 94.5 %copy-start.2 = (s32[1,128]{1,0:T(1,128)S(1)}, s32[1,128]{1,0:T(1,128)}, u32[]{:S(2)}) copy-start(s32[1,128]{1,0:T(1,128)} %param.7) | copy-start | bytes 1540
  22.1 133.3 %copy-start = (bf16[1,2,384,384]{3,2,1,0:T(8,128)(2,1)S(1)}, bf16[1,2,384,384]{3,2,1,0:T(8,128)(2,1)}, u32[]{:S(2)}) copy-start(bf16[1,2,384,384]{3,2,1,0:T(8,128)(2,1)} %param.6) | copy-start | bytes 1769476
  35.4 156.8 %all-gather.4.cloned.1.call-start = ((), (), s32[]{:S(2)}) async-start(), calls=%async_computation.2 | async-start | bytes 9510912 | tf_op jit(solution)/shard_map/all_gather | solution.py:88
Sparse Core Ops, SparseCore 0:
  35.6 81.0 reduce-scatter.1
  120.1 72.1 all-gather.3

commit v2 on v1

v2 whole, which is shorter than its diff:
```python
import functools
import math

import jax
import jax.numpy as jnp
from jax import lax
from jax.experimental import pallas as pl
from jax.experimental.pallas import tpu as pltpu
from jax.sharding import PartitionSpec as P

LX = 64
CAP = 2
RING = 4
CHIPS = RING * RING * RING
PLANE = RING * RING
LANES = 128
BF = jnp.bfloat16
F32 = jnp.float32
MESH = pl.DeviceIdType.MESH

Y, X, Z = 0, 1, 2
CUBE = ((X, 0), (Y, 0), (Z, 0), (X, 1), (Y, 1), (Z, 1))
FACE = ((X, 0), (Z, 0), (X, 1), (Z, 1))


def gray_bit(position, bit):
    return position // 2 if bit else (position % 2 + position // 2) % 2


def across(position, bit):
    return 3 - position if bit else position + 1 - 2 * (position % 2)


def cube_dim(order, stage):
    return CUBE[(order + stage) % 6]


def face_dim(order, stage):
    return FACE[(order + stage) % 4]


def cube_index(place, order):
    return sum(gray_bit(place[a], b) * (1 << s) for s, (a, b) in enumerate(cube_dim(order, s) for s in range(6)))


def face_index(place, order):
    return sum(gray_bit(place[a], b) * (8 >> s) for s, (a, b) in enumerate(face_dim(order, s) for s in range(4)))


def gather_kernel(
    mom,
    vec,
    blk_in,
    own_in,
    picked,
    v,
    vt,
    tab,
    acc,
    full,
    outbox,
    inbox,
    mine,
    every,
    lists,
    ids,
    rows,
    local_sem,
    v_sem,
    list_sem,
    rs_sem,
    ag_sem,
    sib_sem,
    row_sem,
):
    sites, width = v.shape[3], v.shape[4]
    half = width
    rb = width // PLANE
    y = lax.axis_index("tm")
    sp = lax.axis_index("space")
    x, z, k = sp // 8, (sp // 2) % 4, sp % 2
    place = (y, x, z)

    def device(where, core):
        return (where[0], where[1] * 8 + where[2] * 2 + core)

    def neighbour(dim):
        axis, bit = dim
        where = list(place)
        where[axis] = across(place[axis], bit)
        return device(where, k)

    sibling = device(place, 1 - k)

    def remote(src, dst, sems, to):
        return pltpu.make_async_remote_copy(
            src_ref=src, dst_ref=dst, send_sem=sems.at[0], recv_sem=sems.at[1], device_id=to, device_id_type=MESH
        )

    barrier = pltpu.get_barrier_semaphore()
    for dim in CUBE:
        pl.semaphore_signal(barrier, inc=1, device_id=neighbour(dim), device_id_type=MESH)
    pl.semaphore_signal(barrier, inc=1, device_id=sibling, device_id_type=MESH)
    load_v = pltpu.make_async_copy(vec.at[k], v.at[0], local_sem.at[0])
    load_v.start()
    my_cube = [cube_index(place, j) for j in range(6)]
    list_pair = my_cube[0]
    load_blk = pltpu.make_async_copy(blk_in, lists.at[list_pair, k, pl.ds(0, 1)], local_sem.at[1])
    load_own = pltpu.make_async_copy(own_in, lists.at[list_pair, k, pl.ds(1, 1)], local_sem.at[2])
    load_blk.start()
    load_own.start()
    pl.semaphore_wait(barrier, len(CUBE) + 1)

    send_v = remote(vec.at[1 - k], v.at[1], v_sem, sibling)
    send_v.start()
    load_blk.wait()
    load_own.wait()

    def list_copy(stage):
        if stage == 0:
            ref = lists.at[list_pair, k]
            return remote(ref, ref, list_sem.at[:, 0], sibling)
        size = 1 << (stage - 1)
        ref = lists.at[pl.ds(list_pair // size * size, size)]
        return remote(ref, ref, list_sem.at[:, stage], neighbour(cube_dim(0, stage - 1)))

    def list_step(stage):
        if stage > 0:
            list_copy(stage - 1).wait()
        if stage < 7:
            list_copy(stage).start()

    list_step(0)

    lane = lax.broadcasted_iota(jnp.int32, (8, 2 * sites), 1)
    row = lax.broadcasted_iota(jnp.int32, (8, 2 * sites), 0)
    side = lane // sites
    site = (2 * (sp // 2) + jnp.where(side == 0, k, 1 - k)) * sites + lane % sites
    gx, gy, gz = site % LX, site // LX % LX, site // (LX * LX)

    def turns(p):
        return mom[p, 0] * gx + mom[p, 1] * gy + mom[p, 2] * gz

    turn = jnp.where(row < 2, turns(0), turns(1)) - (LX // 4) * (row % 2)
    tab[...] = jnp.transpose(jnp.cos((turn & (LX - 1)).astype(F32) * (2.0 * math.pi / LX)))

    def rs_range(q, stage):
        size = 8 >> stage
        me = face_index(place, q)
        base = me // (2 * size) * (2 * size)
        bit = me // size % 2
        return size, base + bit * size, base + (1 - bit) * size

    def rs_copy(q, stage):
        size, _, other = rs_range(q, stage)
        return remote(
            outbox.at[q, pl.ds(other, size)],
            inbox.at[q, pl.ds(16 - 2 * size, size)],
            rs_sem.at[:, q, stage],
            neighbour(face_dim(q, stage)),
        )

    def rs_finish(q, stage):
        rs_copy(q, stage).wait_recv()
        size, keep, _ = rs_range(q, stage)
        p, h = q // 2, q % 2
        if stage < 3:

            def add(i, carry):
                total = full[q, keep + i] + inbox[q, 16 - 2 * size + i].astype(F32)
                full[q, keep + i] = total
                outbox[q, keep + i] = total.astype(BF)
                return carry

            lax.fori_loop(0, size, add, 0)
            rs_copy(q, stage + 1).start()
        else:
            total = (full[q, keep] + inbox[q, 14].astype(F32)).astype(BF)
            for jj in range(3):
                mine[h * 3 + jj, p] = total[:, jj * LANES : (jj + 1) * LANES]

    for step in range(4):
        s, p = step // 2, step % 2
        if step == 0:
            load_v.wait()
        if step == 2:
            send_v.wait_recv()

        def color(c, carry, s=s, p=p):
            vr, vi = v[s, 0, c], v[s, 1, c]
            if p == 0:
                vt[c, :, :sites] = jnp.transpose(vr)
                vt[c, :, sites:] = jnp.transpose(vi)
            cos = tab[s * sites : (s + 1) * sites, 2 * p : 2 * p + 1]
            sin = tab[s * sites : (s + 1) * sites, 2 * p + 1 : 2 * p + 2]
            fr, fi = vr.astype(F32), vi.astype(F32)
            tr = (cos * fr + sin * fi).astype(BF)
            ti = (cos * fi - sin * fr).astype(BF)
            real = jnp.concatenate([tr, ti], axis=0)
            imag = jnp.concatenate([ti, -tr], axis=0)
            part = jnp.dot(vt[c], jnp.concatenate([real, imag], axis=1), preferred_element_type=F32)
            if s == 0:

                @pl.when(c == 0)
                def _():
                    acc[p] = part

                @pl.when(c != 0)
                def _():
                    acc[p] = acc[p] + part
            else:
                acc[p] = acc[p] + part
            return carry

        lax.fori_loop(0, 3, color, 0)
        list_step(step + 1)
        if s == 1:
            for h in range(2):
                q = p * 2 + h
                for chip in range(PLANE):
                    i = face_index((0, chip // 4, chip % 4), q)
                    tile = acc[p, chip * rb : (chip + 1) * rb, h * half : (h + 1) * half]
                    full[q, i] = tile
                    outbox[q, i] = tile.astype(BF)
                rs_copy(q, 0).start()

    for stage in range(4):
        for q in range(4):
            rs_finish(q, stage)
        if stage < 3:
            list_step(stage + 5)

    def held(j, level):
        size = 1 << level
        return every.at[k, j, pl.ds(my_cube[j] // size * size, size)]

    def other_half(j, level):
        size = 1 << level
        start = my_cube[j] // size
        start = start + 1 - 2 * (start % 2)
        return every.at[k, j, pl.ds(start * size, size)]

    def ag_copy(j, stage, late):
        piece = held if not late else other_half
        ref = piece(j, max(stage - 1, 0))
        return remote(ref, ref, ag_sem.at[:, j, stage, late], neighbour(cube_dim(j, stage)))

    def ag_wait(j, stage):
        size = 1 << stage
        arrived = other_half(j, stage)
        if stage == 0:
            remote(arrived, arrived, ag_sem.at[:, j, 0, 0], sibling).wait_recv()
            return
        for part in range(2):
            piece = every.at[k, j, pl.ds(0, size // 2)]
            remote(piece, piece, ag_sem.at[:, j, stage, part], sibling).wait_recv()

    def sib_copy(j, n):
        ref = held(j, 0) if n == 0 else other_half(j, n - 1)
        return remote(ref, ref, sib_sem.at[:, j, n], sibling)

    for j in range(6):
        every[k, j, my_cube[j]] = mine[j]
        ag_copy(j, 0, 0).start()
        ag_copy(j, 1, 0).start()
        sib_copy(j, 0).start()
    for stage in range(6):
        for j in range(6):
            ag_wait(j, stage)
            if stage < 5:
                ag_copy(j, stage + 1, 1).start()
            if stage < 4:
                ag_copy(j, stage + 2, 0).start()
            sib_copy(j, stage + 1).start()
        if stage == 1:
            me = y * 32 + sp
            at = lax.broadcasted_iota(jnp.int32, (CHIPS, LANES), 1)
            cols = []
            for core in range(2):
                block = lists[:, core, 0, :]
                hit = lists[:, core, 1, :] == me
                first = jnp.min(jnp.where(hit, at, LANES), axis=1, keepdims=True)
                last = jnp.max(jnp.where(hit, at, -1), axis=1, keepdims=True)
                cols.append(jnp.sum(jnp.where(at == first, block + 1, 0), axis=1, keepdims=True) - 1)
                cols.append(
                    jnp.sum(jnp.where((at == last) & (last > first), block + 1, 0), axis=1, keepdims=True) - 1
                )
            table = jnp.full((CHIPS, LANES), -1, jnp.int32)
            for n, col in enumerate(cols):
                table = jnp.where(at == n, col, table)
            ids[...] = table
    for j in range(6):
        for n in range(7):
            sib_copy(j, n).wait_recv()

    out_rows = 2 * CAP * (rb // 2)
    in_rows = 4 * rb
    rho = lax.broadcasted_iota(jnp.int32, (out_rows, in_rows), 0)
    kappa = lax.broadcasted_iota(jnp.int32, (out_rows, in_rows), 1)
    slot, r, core = rho % 2, rho % rb // 2, rho // rb
    target = core * (rb // 2) + r

    def pick(c, carry):
        where = (c // 16, c // 4 % 4, c % 4)
        order = [cube_index(where, j) for j in range(6)]
        bands = []
        for u in range(2):
            for p in range(2):
                bands.append(jnp.concatenate([every[u, j, order[j], p] for j in range(6)], axis=1))
        source = jnp.concatenate(bands, axis=0)
        listed = ids[pl.ds(order[0], 1), :]
        one = jnp.where(slot == 0, listed[:, 0:1], listed[:, 1:2])
        two = jnp.where(slot == 0, listed[:, 2:3], listed[:, 3:4])
        want = jnp.where(core == 0, one, two) * rb + target
        chosen = (kappa == want).astype(F32).astype(BF)
        rows[pl.ds(pl.multiple_of(c * out_rows, out_rows), out_rows), :] = jnp.dot(
            chosen, source, preferred_element_type=F32
        ).astype(BF)
        return carry

    lax.fori_loop(0, CHIPS, pick, 0)
    store = pltpu.make_async_copy(rows, picked, row_sem)
    store.start()

    send_v.wait_send()
    for stage in range(4):
        for q in range(4):
            rs_copy(q, stage).wait_send()
    for j in range(6):
        for stage in range(6):
            for late in range(2 if stage else 1):
                ag_copy(j, stage, late).wait_send()
        for n in range(7):
            sib_copy(j, n).wait_send()
    store.wait()


def product_kernel(rows, pair, out, kernel):
    width = pair.shape[1]

    @pl.when(pl.program_id(0) == 0)
    def _():
        kernel[:width, :width] = pair[0]
        kernel[:width, width:] = pair[1]
        kernel[width:, :width] = -pair[1]
        kernel[width:, width:] = pair[0]

    y = jnp.dot(rows[...], kernel[...], preferred_element_type=F32).astype(BF)
    out[...] = y.reshape(out.shape)


def body(vectors, perambulators, item_block, item_owner, momenta):
    sites, width = vectors.shape[3], vectors.shape[4]
    devices = 2 * CHIPS
    rb = width // PLANE
    total = devices * CAP * (rb // 2)
    anywhere = pl.BlockSpec(memory_space=pl.ANY)
    picked = pl.pallas_call(
        gather_kernel,
        out_shape=jax.ShapeDtypeStruct((total, 2 * width), BF),
        in_specs=[pl.BlockSpec(memory_space=pltpu.SMEM), anywhere, anywhere, anywhere],
        out_specs=anywhere,
        scratch_shapes=[
            pltpu.VMEM((2, 2, 3, sites, width), BF),
            pltpu.VMEM((3, width, 2 * sites), BF),
            pltpu.VMEM((2 * sites, 8), F32),
            pltpu.VMEM((2, width, 2 * width), F32),
            pltpu.VMEM((4, PLANE, rb, width), F32),
            pltpu.VMEM((4, PLANE, rb, width), BF),
            pltpu.VMEM((4, PLANE, rb, width), BF),
            pltpu.VMEM((6, 2, rb, LANES), BF),
            pltpu.VMEM((2, 6, CHIPS, 2, rb, LANES), BF),
            pltpu.VMEM((CHIPS, 2, 2, LANES), jnp.int32),
            pltpu.VMEM((CHIPS, LANES), jnp.int32),
            pltpu.VMEM((total, 2 * width), BF),
            pltpu.SemaphoreType.DMA((3,)),
            pltpu.SemaphoreType.DMA((2,)),
            pltpu.SemaphoreType.DMA((2, 7)),
            pltpu.SemaphoreType.DMA((2, 4, 4)),
            pltpu.SemaphoreType.DMA((2, 6, 6, 2)),
            pltpu.SemaphoreType.DMA((2, 6, 7)),
            pltpu.SemaphoreType.DMA,
        ],
        compiler_params=pltpu.CompilerParams(
            collective_id=0, has_side_effects=True, vmem_limit_bytes=56 * 1024 * 1024
        ),
        name="gather_elementals",
    )(momenta, vectors, item_block, item_owner)
    tile = 384
    out = pl.pallas_call(
        product_kernel,
        out_shape=jax.ShapeDtypeStruct((total // 2, 2, 2 * width), BF),
        grid=(total // tile,),
        in_specs=[
            pl.BlockSpec((tile, 2 * width), lambda i: (i, 0)),
            pl.BlockSpec((2, width, width), lambda i: (0, 0, 0)),
        ],
        out_specs=pl.BlockSpec((tile // 2, 2, 2 * width), lambda i: (i, 0, 0)),
        scratch_shapes=[pltpu.VMEM((2 * width, 2 * width), BF)],
        compiler_params=pltpu.CompilerParams(vmem_limit_bytes=32 * 1024 * 1024),
        name="contract_perambulators",
    )(picked, perambulators[0])
    return out.reshape(1, devices, rb // 2, CAP, 2 * width).transpose(0, 1, 3, 2, 4)


def solution(mesh):
    both = ("tm", "space")
    in_specs = (
        P("tm", None, None, "space", None),
        P(both, None, None, None),
        P(both, None),
        P(both, None),
        P(),
    )
    out_specs = P(both, None, None, None, None)
    return jax.shard_map(body, mesh=mesh, in_specs=in_specs, out_specs=out_specs, check_vma=False)
```

time: 269 us -> 99.5 us (0.37)
  waiting for transfers between devices: 118 us -> 0 us
  Pallas kernels: 0 us -> 97 us
  local copies, waits for them, and re-layouts: 61.9 us -> 2.33 us
  blocking collectives: 37.4 us -> 0 us
  matrix products: 22.1 us -> 0 us
  other arithmetic: 14.6 us -> 0 us
  between operations: 13.6 us -> 0.03 us
    pallas_call x0 -> x2, Pallas kernels: none -> 97 us  [the longest x1 90.4 us: body(): pl.pallas_call(gather_kernel, out_shape=jax.ShapeDtypeStruct((total, 2 *...]
    reduce_scatter x1 -> x0, waiting for transfers between devices: 81.1 us -> none  [body(): blocks = lax.psum_scatter(flat, SPACE, scatter_dimension=0, tiled=True)]
    all_gather x1 -> x0, blocking collectives: 37.4 us -> none  [body(): lax.all_gather(jnp.concatenate([item_block, item_owner], axis=0), TM_SPACE)]
    all_gather x1 -> x0, waiting for transfers between devices: 36.7 us -> none  [body(): lax.all_gather(blocks, TM_SPACE, tiled=True)]
    dot_general x3 -> x0, matrix products: 22.1 us -> none  [the longest x1 13.3 us: body(): jnp.einsum('tmk,tpmj->tpkj', left_side, right_side, preferred_element_typ...]
    another operation x2 -> x0, local copies, waits for them, and re-layouts: 16.9 us -> none  [body(): return result[None]]
    gather x2 -> x0, local copies, waits for them, and re-layouts: 16.5 us -> none  [body(): received = jnp.take(padded, rows.reshape(-1), axis=0)]
    reshape x1 -> x0, local copies, waits for them, and re-layouts: 15.3 us -> none  [body(): lax.all_gather(blocks, TM_SPACE, tiled=True)]
  transfers between devices with their start and end apart: 2 -> 0, of which waited for: 2 -> 0; matrix products, arithmetic and copies ran while one was open for 1% -> 0% of each run, Pallas kernels for 0% -> 0%
where the time goes in v2:
time: 99.5 us; the launch traced here: 99.3 us
  Pallas kernels  97 us (97%)
  local copies, waits for them, and re-layouts  2.33 us (2%)
    pallas_call x1, Pallas kernels, body(): pl.pallas_call(gather_kernel, out_shape=jax.ShapeDtypeStruct((total, 2 *...  90.4 us
    pallas_call x1, Pallas kernels, body(): pl.pallas_call(product_kernel, out_shape=jax.ShapeDtypeStruct((total // 2...  6.62 us
    unnamed x4, local copies, waits for them, and re-layouts  2.33 us

profile of v2, /device:TPU:1, one launch (start us, length us, event | category | flops | bytes accessed | tf_op | source)
XLA Modules:
  0.0 99.3 jit_solution(11882694422436558527)
XLA Ops:
  0.0 0.0 copy-start.1
  0.0 90.4 %gather_elementals.1.rows = bf16[3072,768]{1,0:T(8,128)(2,1)} custom-call(s32[2,3]{1,0:T(2,128)} %mom.1, bf16[2,2,3,512,384]{4,3,2,1,0:T(8,128)(2,1)} %vec.1, s32[1,128]{1,0:T(1,128)} %blk_in.1, s32[1,128]{1,0:T(1,128)} %own_in.1), custom_call_target="tpu_custom_call" | custom-call | tf_op jit(solution)/shard_map/gather_elementals/pallas_call | solution.py:358
  90.4 0.0 copy-done.1
  90.4 0.0 copy-start
  90.4 2.3 %copy-done = bf16[3072,768]{1,0:T(8,128)(2,1)S(1)} copy-done((bf16[3072,768]{1,0:T(8,128)(2,1)S(1)}, bf16[3072,768]{1,0:T(8,128)(2,1)}, u32[]{:S(2)}) %copy-start) | copy-done | bytes 4718616
  92.7 6.6 %contract_perambulators.1 = bf16[1536,2,768]{2,1,0:T(2,128)(2,1)} custom-call(bf16[3072,768]{1,0:T(8,128)(2,1)S(1)} %copy-done, bf16[2,384,384]{2,1,0:T(8,128)(2,1)S(1)} %bitcast.4), custom_call_target="tpu_custom_call" | custom-call | tf_op jit(solution)/shard_map/contract_perambulators/pallas_call | solution.py:390
Async XLA Ops:
  0.0 90.4 %copy-start.1 = (bf16[1,2,384,384]{3,2,1,0:T(8,128)(2,1)S(1)}, bf16[1,2,384,384]{3,2,1,0:T(8,128)(2,1)}, u32[]{:S(2)}) copy-start(bf16[1,2,384,384]{3,2,1,0:T(8,128)(2,1)} %param.6) | copy-start | bytes 1769476
  90.4 2.3 %copy-start = (bf16[3072,768]{1,0:T(8,128)(2,1)S(1)}, bf16[3072,768]{1,0:T(8,128)(2,1)}, u32[]{:S(2)}) copy-start(bf16[3072,768]{1,0:T(8,128)(2,1)} %gather_elementals.1.rows) | copy-start | bytes 14155780

commit v3 on v2

v3 whole, which is shorter than its diff:
```python
import math

import jax
import jax.numpy as jnp
from jax import lax
from jax.experimental import pallas as pl
from jax.experimental.pallas import tpu as pltpu
from jax.sharding import PartitionSpec as P

LX = 64
CAP = 2
RING = 4
CHIPS = RING * RING * RING
PLANE = RING * RING
LANES = 128
BF = jnp.bfloat16
F32 = jnp.float32
MESH = pl.DeviceIdType.MESH

Y, X, Z = 0, 1, 2
REDUCE_AXES = ((X, Z), (Z, X), (X, Z), (Z, X), (X, Z), (Z, X))
GATHER_AXES = ((Y, X, Z), (X, Z, Y), (Z, Y, X), (Y, Z, X), (X, Y, Z), (Z, X, Y))
LIST_AXES = (X, Z, Y)


def plane_index(place, j):
    a, b = REDUCE_AXES[j]
    return place[a] * 4 + place[b]


def chip_index(place, axes):
    a, b, c = axes
    return place[c] * 16 + place[b] * 4 + place[a]


def gather_kernel(
    mom,
    vec,
    blk_in,
    own_in,
    picked,
    v,
    vt,
    vn,
    tw,
    tab,
    core_out,
    core_in,
    full,
    outbox,
    inbox,
    inbox2,
    every,
    lists,
    ids,
    rows,
    local_sem,
    core_sem,
    list_sem,
    rs_sem,
    ag_sem,
    last_sem,
    fwd_sem,
    sib_sem,
    row_sem,
):
    sites, width = v.shape[3], v.shape[4]
    colors = v.shape[2]
    rb = 2 * width // PLANE
    y = lax.axis_index("tm")
    sp = lax.axis_index("space")
    x, z, k = sp // 8, (sp // 2) % 4, sp % 2
    place = (y, x, z)

    def device(where, core):
        return (where[0], where[1] * 8 + where[2] * 2 + core)

    def ring(axis, offset):
        where = list(place)
        where[axis] = (place[axis] + offset) % RING
        return where[axis], device(where, k)

    sibling = device(place, 1 - k)

    def remote(src, dst, sems, to):
        return pltpu.make_async_remote_copy(
            src_ref=src, dst_ref=dst, send_sem=sems.at[0], recv_sem=sems.at[1], device_id=to, device_id_type=MESH
        )

    barrier = pltpu.get_barrier_semaphore()
    for axis in (Y, X, Z):
        for offset in (1, 2, 3):
            pl.semaphore_signal(barrier, inc=1, device_id=ring(axis, offset)[1], device_id_type=MESH)
    pl.semaphore_signal(barrier, inc=1, device_id=sibling, device_id_type=MESH)

    def load(n, c):
        slab = (1 - k) if n == 0 else k
        return pltpu.make_async_copy(vec.at[slab, :, c], v.at[n, :, c], local_sem.at[n * colors + c])

    for n in range(2):
        for c in range(colors):
            load(n, c).start()
    my_list = chip_index(place, LIST_AXES)
    load_blk = pltpu.make_async_copy(blk_in, lists.at[my_list, k, pl.ds(0, 1)], local_sem.at[2 * colors])
    load_own = pltpu.make_async_copy(own_in, lists.at[my_list, k, pl.ds(1, 1)], local_sem.at[2 * colors + 1])
    load_blk.start()
    load_own.start()

    def list_copies(stage):
        if stage == 0:
            ref = lists.at[my_list, k]
            return [remote(ref, ref, list_sem.at[:, 0, 0], sibling)]
        size = 4 ** (stage - 1)
        ref = lists.at[pl.ds(my_list // size * size, size)]
        axis = LIST_AXES[stage - 1]
        return [remote(ref, ref, list_sem.at[:, stage, o - 1], ring(axis, o)[1]) for o in (1, 2, 3)]

    def list_step(stage):
        if stage > 0:
            for copy in list_copies(stage - 1):
                copy.wait()
        if stage < 4:
            for copy in list_copies(stage):
                copy.start()

    lane = lax.broadcasted_iota(jnp.int32, (8, sites), 1)
    row = lax.broadcasted_iota(jnp.int32, (8, sites), 0)
    site = sp * sites + lane
    gx, gy, gz = site % LX, site // LX % LX, site // (LX * LX)

    def turns(p):
        return mom[p, 0] * gx + mom[p, 1] * gy + mom[p, 2] * gz

    turn = jnp.where(row < 2, turns(0), turns(1)) - (LX // 4) * (row % 2)
    tab[...] = jnp.transpose(jnp.cos((turn & (LX - 1)).astype(F32) * (2.0 * math.pi / LX)))

    def twist(n):
        def color(c, carry):
            vr, vi = v[n, 0, c], v[n, 1, c]
            tr, ti = jnp.transpose(vr), jnp.transpose(vi)
            vt[c, :, :sites] = tr
            vt[c, :, sites:] = ti
            vn[c, :, :sites] = -ti
            vn[c, :, sites:] = tr
            fr, fi = vr.astype(F32), vi.astype(F32)
            for p in range(2):
                cos = tab[:, 2 * p : 2 * p + 1]
                sin = tab[:, 2 * p + 1 : 2 * p + 2]
                tw[c, :sites, p * width : (p + 1) * width] = (cos * fr + sin * fi).astype(BF)
                tw[c, sites:, p * width : (p + 1) * width] = (cos * fi - sin * fr).astype(BF)
            return carry

        for c in range(colors):
            load(n, c).wait()
        lax.fori_loop(0, colors, color, 0)

    def product(h):
        left = vn if h else vt
        total = jnp.dot(left[0], tw[0], preferred_element_type=F32)
        for c in range(1, colors):
            total = total + jnp.dot(left[c], tw[c], preferred_element_type=F32)
        return total

    def piece(total, chip):
        p, i = chip // (PLANE // 2), chip % (PLANE // 2)
        return total[i * rb : (i + 1) * rb, p * width : (p + 1) * width]

    def core_copy(h):
        return remote(core_out.at[h], core_in.at[h], core_sem.at[:, h], sibling)

    def rs1_copies(j):
        copies = []
        for o in (1, 2, 3):
            at, to = ring(REDUCE_AXES[j][0], o)
            copies.append(
                remote(outbox.at[j, pl.ds(at * 4, 4)], inbox.at[j, o - 1], rs_sem.at[:, j, 0, o - 1], to)
            )
        return copies

    def rs2_copies(j):
        copies = []
        for o in (1, 2, 3):
            at, to = ring(REDUCE_AXES[j][1], o)
            row_of = place[REDUCE_AXES[j][0]] * 4 + at
            copies.append(remote(outbox.at[j, row_of], inbox2.at[j, o - 1], rs_sem.at[:, j, 1, o - 1], to))
        return copies

    def rs1_start(j):
        for copy in rs1_copies(j):
            copy.start()

    def rs1_finish(j):
        for copy in rs1_copies(j):
            copy.wait_recv()
        base = place[REDUCE_AXES[j][0]] * 4
        for b in range(4):
            total = full[j, base + b]
            for o in range(3):
                total = total + inbox[j, o, b].astype(F32)
            full[j, base + b] = total
            outbox[j, base + b] = total.astype(BF)
        for copy in rs2_copies(j):
            copy.start()

    def rs2_finish(j):
        for copy in rs2_copies(j):
            copy.wait_recv()
        total = full[j, plane_index(place, j)]
        for o in range(3):
            total = total + inbox2[j, o].astype(F32)
        every[k, j, my_chip[j]] = total.astype(BF)

    my_chip = [chip_index(place, axes) for axes in GATHER_AXES]

    def block(j, start, size):
        return every.at[k, j, pl.ds(start, size)]

    def group(j, c, b):
        return block(j, c * 16 + b * 4, 4)

    def coords(j):
        a, b, c = GATHER_AXES[j]
        return place[a], place[b], place[c]

    def ag1_copies(j):
        ref = block(j, my_chip[j], 1)
        return [remote(ref, ref, ag_sem.at[:, j, 0, o - 1], ring(GATHER_AXES[j][0], o)[1]) for o in (1, 2, 3)]

    def ag2_copies(j):
        _, b, c = coords(j)
        ref = group(j, c, b)
        return [remote(ref, ref, ag_sem.at[:, j, 1, o - 1], ring(GATHER_AXES[j][1], o)[1]) for o in (1, 2, 3)]

    def ag3_copy(j, g, way):
        _, b, c = coords(j)
        ref = group(j, c, (b + g) % RING)
        return remote(ref, ref, last_sem.at[:, j, g, way], ring(GATHER_AXES[j][2], 1 if way == 0 else 3)[1])

    def fwd_copy(j, g):
        _, b, c = coords(j)
        way = g // 2
        source = (c + (3 if way == 0 else 1)) % RING
        ref = group(j, source, (b + g) % RING)
        return remote(ref, ref, fwd_sem.at[:, j, g], ring(GATHER_AXES[j][2], 1 if way == 0 else 3)[1])

    def sib_copy(j, n):
        _, b, c = coords(j)
        if n < 4:
            ref = group(j, c, (b + n) % RING)
        elif n < 6:
            ref = block(j, (c + (3 if n == 4 else 1)) % RING * 16, 16)
        else:
            ref = block(j, (c + 2) % RING * 16, 16)
        return remote(ref, ref, sib_sem.at[:, j, n], sibling)

    def ag1_start(j):
        for copy in ag1_copies(j):
            copy.start()

    def ag1_finish(j):
        for copy in ag1_copies(j):
            copy.wait_recv()
        for copy in ag2_copies(j):
            copy.start()
        for way in range(2):
            ag3_copy(j, 0, way).start()
        sib_copy(j, 0).start()

    def ag2_finish(j):
        for o, copy in zip((1, 2, 3), ag2_copies(j)):
            copy.wait_recv()
            g = 4 - o
            for way in range(2):
                ag3_copy(j, g, way).start()
            sib_copy(j, g).start()

    def ag3_finish(j):
        for g in range(4):
            ag3_copy(j, g, g // 2).wait_recv()
            fwd_copy(j, g).start()
        for g in range(4):
            ag3_copy(j, g, 1 - g // 2).wait_recv()
        sib_copy(j, 4).start()
        sib_copy(j, 5).start()

    def ag4_finish(j):
        for g in range(4):
            fwd_copy(j, g).wait_recv()
        sib_copy(j, 6).start()

    twist(0)
    for h in range(2):
        total = product(h)
        for chip in range(PLANE):
            core_out[h, chip] = piece(total, chip).astype(BF)
        if h == 0:
            pl.semaphore_wait(barrier, 10)
            load_blk.wait()
            load_own.wait()
        core_copy(h).start()
        list_step(h)
    twist(1)
    for h in range(2):
        total = product(h)
        core_copy(h).wait_recv()
        for chip in range(PLANE):
            both = piece(total, chip) + core_in[h, chip].astype(F32)
            for jj in range(3):
                j = h * 3 + jj
                i = plane_index((0, chip // 4, chip % 4), j)
                tile = both[:, jj * LANES : (jj + 1) * LANES]
                full[j, i] = tile
                outbox[j, i] = tile.astype(BF)
        for jj in range(3):
            rs1_start(h * 3 + jj)
        list_step(h + 2)
    for j in range(6):
        rs1_finish(j)
    for j in range(6):
        rs2_finish(j)
        ag1_start(j)
    list_step(4)

    me = y * 32 + sp
    at = lax.broadcasted_iota(jnp.int32, (CHIPS, LANES), 1)
    table = jnp.full((CHIPS, LANES), -1, jnp.int32)
    for core in range(2):
        listed = lists[:, core, 0, :] + 1
        hit = lists[:, core, 1, :] == me
        first = jnp.min(jnp.where(hit, at, LANES), axis=1, keepdims=True)
        last = jnp.max(jnp.where(hit, at, -1), axis=1, keepdims=True)
        one = jnp.sum(jnp.where(at == first, listed, 0), axis=1, keepdims=True) - 1
        two = jnp.sum(jnp.where((at == last) & (last > first), listed, 0), axis=1, keepdims=True) - 1
        table = jnp.where(at == 2 * core, one, jnp.where(at == 2 * core + 1, two, table))
    ids[...] = table

    for j in range(6):
        ag1_finish(j)
    for j in range(6):
        ag2_finish(j)
    for j in range(6):
        ag3_finish(j)
    for j in range(6):
        ag4_finish(j)
    for j in range(6):
        for n in range(7):
            sib_copy(j, n).wait_recv()

    own_rows = rb // 4
    out_rows = 4 * CAP * own_rows
    in_rows = 4 * rb
    rho = lax.broadcasted_iota(jnp.int32, (out_rows, in_rows), 0)
    kappa = lax.broadcasted_iota(jnp.int32, (out_rows, in_rows), 1)
    dev = rho // (CAP * own_rows)
    target = dev * own_rows + rho // CAP % own_rows
    which = dev * CAP + rho % CAP

    def pick(n, carry):
        gy_, g = n // 8, n % 8
        bands = []
        for u in range(2):
            for p in range(2):
                where = (gy_, p * 2 + g // 4, g % 4)
                bands.append(
                    jnp.concatenate([every[u, j, chip_index(where, GATHER_AXES[j])] for j in range(6)], axis=1)
                )
        source = jnp.concatenate(bands, axis=0)
        want = target
        for half in range(2):
            chip = chip_index((gy_, g // 2, g % 2 * 2 + half), LIST_AXES)
            listed = ids[pl.ds(chip, 1), :]
            for lane_ in range(4):
                want = jnp.where(which == half * 4 + lane_, target + listed[:, lane_ : lane_ + 1] * rb, want)
        chosen = (kappa == want).astype(F32).astype(BF)
        rows[pl.ds(pl.multiple_of(n * out_rows, out_rows), out_rows), :] = jnp.dot(
            chosen, source, preferred_element_type=F32
        ).astype(BF)
        return carry

    lax.fori_loop(0, CHIPS // 2, pick, 0)
    store = pltpu.make_async_copy(rows, picked, row_sem)
    store.start()

    for h in range(2):
        core_copy(h).wait_send()
    for j in range(6):
        for copy in rs1_copies(j) + rs2_copies(j) + ag1_copies(j) + ag2_copies(j):
            copy.wait_send()
        for g in range(4):
            for way in range(2):
                ag3_copy(j, g, way).wait_send()
            fwd_copy(j, g).wait_send()
        for g in range(4):
            pass
        for n in range(7):
            sib_copy(j, n).wait_send()
    store.wait()


def product_kernel(rows, pair, out, kernel):
    width = pair.shape[1]

    @pl.when(pl.program_id(0) == 0)
    def _():
        kernel[:width, :width] = pair[0]
        kernel[:width, width:] = pair[1]
        kernel[width:, :width] = -pair[1]
        kernel[width:, width:] = pair[0]

    y = jnp.dot(rows[...], kernel[...], preferred_element_type=F32).astype(BF)
    out[...] = y.reshape(out.shape)


def body(vectors, perambulators, item_block, item_owner, momenta):
    colors, sites, width = vectors.shape[2:]
    devices = 2 * CHIPS
    rb = 2 * width // PLANE
    own_rows = rb // 4
    total = devices * CAP * own_rows
    anywhere = pl.BlockSpec(memory_space=pl.ANY)
    picked = pl.pallas_call(
        gather_kernel,
        out_shape=jax.ShapeDtypeStruct((total, 2 * width), BF),
        in_specs=[pl.BlockSpec(memory_space=pltpu.SMEM), anywhere, anywhere, anywhere],
        out_specs=anywhere,
        scratch_shapes=[
            pltpu.VMEM((2, 2, colors, sites, width), BF),
            pltpu.VMEM((colors, width, 2 * sites), BF),
            pltpu.VMEM((colors, width, 2 * sites), BF),
            pltpu.VMEM((colors, 2 * sites, 2 * width), BF),
            pltpu.VMEM((sites, 8), F32),
            pltpu.VMEM((2, PLANE, rb, width), BF),
            pltpu.VMEM((2, PLANE, rb, width), BF),
            pltpu.VMEM((6, PLANE, rb, LANES), F32),
            pltpu.VMEM((6, PLANE, rb, LANES), BF),
            pltpu.VMEM((6, 3, 4, rb, LANES), BF),
            pltpu.VMEM((6, 3, rb, LANES), BF),
            pltpu.VMEM((2, 6, CHIPS, rb, LANES), BF),
            pltpu.VMEM((CHIPS, 2, 2, LANES), jnp.int32),
            pltpu.VMEM((CHIPS, LANES), jnp.int32),
            pltpu.VMEM((total, 2 * width), BF),
            pltpu.SemaphoreType.DMA((2 * colors + 2,)),
            pltpu.SemaphoreType.DMA((2, 2)),
            pltpu.SemaphoreType.DMA((2, 4, 3)),
            pltpu.SemaphoreType.DMA((2, 6, 2, 3)),
            pltpu.SemaphoreType.DMA((2, 6, 2, 3)),
            pltpu.SemaphoreType.DMA((2, 6, 4, 2)),
            pltpu.SemaphoreType.DMA((2, 6, 4)),
            pltpu.SemaphoreType.DMA((2, 6, 7)),
            pltpu.SemaphoreType.DMA,
        ],
        compiler_params=pltpu.CompilerParams(
            collective_id=0, has_side_effects=True, vmem_limit_bytes=56 * 1024 * 1024
        ),
        name="gather_elementals",
    )(momenta, vectors, item_block, item_owner)
    tile = 384
    out = pl.pallas_call(
        product_kernel,
        out_shape=jax.ShapeDtypeStruct((total // 2, 2, 2 * width), BF),
        grid=(total // tile,),
        in_specs=[
            pl.BlockSpec((tile, 2 * width), lambda i: (i, 0)),
            pl.BlockSpec((2, width, width), lambda i: (0, 0, 0)),
        ],
        out_specs=pl.BlockSpec((tile // 2, 2, 2 * width), lambda i: (i, 0, 0)),
        scratch_shapes=[pltpu.VMEM((2 * width, 2 * width), BF)],
        compiler_params=pltpu.CompilerParams(vmem_limit_bytes=56 * 1024 * 1024),
        name="contract_perambulators",
    )(picked, perambulators[0])
    return out.reshape(1, devices, own_rows, CAP, 2 * width).transpose(0, 1, 3, 2, 4)


def solution(mesh):
    both = ("tm", "space")
    in_specs = (
        P("tm", None, None, "space", None),
        P(both, None, None, None),
        P(both, None),
        P(both, None),
        P(),
    )
    out_specs = P(both, None, None, None, None)
    return jax.shard_map(body, mesh=mesh, in_specs=in_specs, out_specs=out_specs, check_vma=False)
```

time: 99.5 us -> 86 us (0.86)
  Pallas kernels: 97 us -> 85.7 us
  local copies, waits for them, and re-layouts: 2.33 us -> 0 us
    pallas_call x1, Pallas kernels: 90.4 us -> 76.3 us  [body(): pl.pallas_call(gather_kernel, out_shape=jax.ShapeDtypeStruct((total, 2 *...]
    pallas_call x1, Pallas kernels: 6.62 us -> 9.43 us  [body(): pl.pallas_call(product_kernel, out_shape=jax.ShapeDtypeStruct((total // 2...]
    unnamed x4 -> x0, local copies, waits for them, and re-layouts: 2.33 us -> none
where the time goes in v3:
time: 86 us; the launch traced here: 85.7 us
  Pallas kernels  85.7 us (100%)
    pallas_call x1, Pallas kernels, body(): pl.pallas_call(gather_kernel, out_shape=jax.ShapeDtypeStruct((total, 2 *...  76.3 us
    pallas_call x1, Pallas kernels, body(): pl.pallas_call(product_kernel, out_shape=jax.ShapeDtypeStruct((total // 2...  9.43 us

profile of v3, /device:TPU:1, one launch (start us, length us, event | category | flops | bytes accessed | tf_op | source)
XLA Modules:
  0.0 85.7 jit_solution(14307761195354201520)
XLA Ops:
  0.0 76.3 %gather_elementals.1.rows = bf16[3072,768]{1,0:T(8,128)(2,1)} custom-call(s32[2,3]{1,0:T(2,128)} %mom.1, bf16[2,2,3,512,384]{4,3,2,1,0:T(8,128)(2,1)} %vec.1, s32[1,128]{1,0:T(1,128)} %blk_in.1, s32[1,128]{1,0:T(1,128)} %own_in.1), custom_call_target="tpu_custom_call" | custom-call | tf_op jit(solution)/shard_map/gather_elementals/pallas_call | solution.py:421
  76.3 9.4 %contract_perambulators.1 = bf16[1536,2,768]{2,1,0:T(2,128)(2,1)} custom-call(bf16[3072,768]{1,0:T(8,128)(2,1)} %gather_elementals.1.rows, bf16[2,384,384]{2,1,0:T(8,128)(2,1)} %bitcast.4), custom_call_target="tpu_custom_call" | custom-call | tf_op jit(solution)/shard_map/contract_perambulators/pallas_call | solution.py:458

commit v4 on v3

--- a/solution.py
+++ b/solution.py
@@ -19,8 +19,10 @@
 
 Y, X, Z = 0, 1, 2
 REDUCE_AXES = ((X, Z), (Z, X), (X, Z), (Z, X), (X, Z), (Z, X))
-GATHER_AXES = ((Y, X, Z), (X, Z, Y), (Z, Y, X), (Y, Z, X), (X, Y, Z), (Z, X, Y))
-LIST_AXES = (X, Z, Y)
+GATHER_AXES = ((X, Z, Y), (Y, Z, X), (X, Z, Y), (X, Y, Z), (X, Z, Y), (Z, Y, X))
+LIST_AXES = (Z, X, Y)
+STAGE_AT = (0.0, 2.2, 5.6, 8.7, 12.2, 15.7, 20.7, 24.2)
+CHOOSE_AT = 21.3
 
 
 def plane_index(place, j):
@@ -53,6 +55,7 @@
     every,
     lists,
     ids,
+    chosen,
     rows,
     local_sem,
     core_sem,
@@ -135,35 +138,35 @@
     tab[...] = jnp.transpose(jnp.cos((turn & (LX - 1)).astype(F32) * (2.0 * math.pi / LX)))
 
     def twist(n):
-        def color(c, carry):
+        for c in range(colors):
+            load(n, c).wait()
+            low, mid, high = 2 * c * sites, (2 * c + 1) * sites, (2 * c + 2) * sites
             vr, vi = v[n, 0, c], v[n, 1, c]
             tr, ti = jnp.transpose(vr), jnp.transpose(vi)
-            vt[c, :, :sites] = tr
-            vt[c, :, sites:] = ti
-            vn[c, :, :sites] = -ti
-            vn[c, :, sites:] = tr
+            vt[n, :, low:mid] = tr
+            vt[n, :, mid:high] = ti
+            vn[n, :, low:mid] = -ti
+            vn[n, :, mid:high] = tr
             fr, fi = vr.astype(F32), vi.astype(F32)
             for p in range(2):
                 cos = tab[:, 2 * p : 2 * p + 1]
                 sin = tab[:, 2 * p + 1 : 2 * p + 2]
-                tw[c, :sites, p * width : (p + 1) * width] = (cos * fr + sin * fi).astype(BF)
-                tw[c, sites:, p * width : (p + 1) * width] = (cos * fi - sin * fr).astype(BF)
-            return carry
-
-        for c in range(colors):
-            load(n, c).wait()
-        lax.fori_loop(0, colors, color, 0)
-
-    def product(h):
-        left = vn if h else vt
-        total = jnp.dot(left[0], tw[0], preferred_element_type=F32)
-        for c in range(1, colors):
-            total = total + jnp.dot(left[c], tw[c], preferred_element_type=F32)
-        return total
-
-    def piece(total, chip):
-        p, i = chip // (PLANE // 2), chip % (PLANE // 2)
-        return total[i * rb : (i + 1) * rb, p * width : (p + 1) * width]
+                real = (cos * fr + sin * fi).astype(BF)
+                imag = (cos * fi - sin * fr).astype(BF)
+                for jj in range(3):
+                    cols = slice(jj * LANES, (jj + 1) * LANES)
+                    tw[n, jj, low:mid, p * LANES : (p + 1) * LANES] = real[:, cols]
+                    tw[n, jj, mid:high, p * LANES : (p + 1) * LANES] = imag[:, cols]
+
+    def product(n, j):
+        left = vn if j // 3 else vt
+        return jnp.dot(left[n], tw[n, j % 3], preferred_element_type=F32)
+
+    def pieces(j):
+        for chip in range(PLANE):
+            p, i = chip // (PLANE // 2), chip % (PLANE // 2)
+            at = plane_index((0, chip // 4, chip % 4), j)
+            yield at, slice(i * rb, (i + 1) * rb), slice(p * LANES, (p + 1) * LANES)
 
     def core_copy(h):
         return remote(core_out.at[h], core_in.at[h], core_sem.at[:, h], sibling)
@@ -288,74 +291,84 @@
             fwd_copy(j, g).wait_recv()
         sib_copy(j, 6).start()
 
-    twist(0)
-    for h in range(2):
-        total = product(h)
-        for chip in range(PLANE):
-            core_out[h, chip] = piece(total, chip).astype(BF)
-        if h == 0:
+    def make_table():
+        me = y * 32 + sp
+        at = lax.broadcasted_iota(jnp.int32, (CHIPS, LANES), 1)
+        table = jnp.full((CHIPS, LANES), -1, jnp.int32)
+        for core in range(2):
+            listed = lists[:, core, 0, :] + 1
+            hit = lists[:, core, 1, :] == me
+            first = jnp.min(jnp.where(hit, at, LANES), axis=1, keepdims=True)
+            last = jnp.max(jnp.where(hit, at, -1), axis=1, keepdims=True)
+            one = jnp.sum(jnp.where(at == first, listed, 0), axis=1, keepdims=True) - 1
+            two = jnp.sum(jnp.where((at == last) & (last > first), listed, 0), axis=1, keepdims=True) - 1
+            table = jnp.where(at == 2 * core, one, jnp.where(at == 2 * core + 1, two, table))
+        ids[...] = table
+
+
+    own_rows = rb // 4
+    out_rows = 4 * CAP * own_rows
+    in_rows = 4 * rb
+    rho = lax.broadcasted_iota(jnp.int32, (out_rows, CHIPS // 2), 0)
+    kappa = lax.broadcasted_iota(jnp.int32, (out_rows, in_rows), 1).astype(F32)
+    target = rho // (CAP * own_rows) * own_rows + rho // CAP % own_rows
+
+    def choose_all():
+        make_table()
+        lane_ = lax.broadcasted_iota(jnp.int32, (out_rows, LANES), 1)
+        row_ = lax.broadcasted_iota(jnp.int32, (out_rows, LANES), 0)
+        which = row_ // (CAP * own_rows) * CAP + row_ % CAP
+        want = target.astype(F32)
+        for half in range(2):
+            spread = jnp.where(which == half * 4 + lane_, jnp.where(lane_ < 4, rb, 0), 0).astype(F32).astype(BF)
+            some = ids[pl.ds(half, CHIPS // 2, stride=2), :].astype(F32).astype(BF)
+            want = want + lax.dot_general(spread, some, (((1,), (1,)), ((), ())), preferred_element_type=F32)
+        for n in range(CHIPS // 2):
+            chosen[n] = (kappa == want[:, n : n + 1]).astype(F32).astype(BF)
+
+    def dots(j):
+        total = product(0, j)
+        for at, r, c in pieces(j):
+            core_out[j, at] = total[r, c].astype(BF)
+        total = product(1, j)
+        for at, r, c in pieces(j):
+            full[j, at] = total[r, c]
+        if j == 0:
             pl.semaphore_wait(barrier, 10)
-            load_blk.wait()
-            load_own.wait()
-        core_copy(h).start()
-        list_step(h)
-    twist(1)
-    for h in range(2):
-        total = product(h)
-        core_copy(h).wait_recv()
-        for chip in range(PLANE):
-            both = piece(total, chip) + core_in[h, chip].astype(F32)
-            for jj in range(3):
-                j = h * 3 + jj
-                i = plane_index((0, chip // 4, chip % 4), j)
-                tile = both[:, jj * LANES : (jj + 1) * LANES]
-                full[j, i] = tile
-                outbox[j, i] = tile.astype(BF)
-        for jj in range(3):
-            rs1_start(h * 3 + jj)
-        list_step(h + 2)
-    for j in range(6):
-        rs1_finish(j)
-    for j in range(6):
+        core_copy(j).start()
+
+    def core_finish(j):
+        core_copy(j).wait_recv()
+        total = full[j] + core_in[j].astype(F32)
+        full[j] = total
+        outbox[j] = total.astype(BF)
+        rs1_start(j)
+
+    def reduce_finish(j):
         rs2_finish(j)
         ag1_start(j)
-    list_step(4)
-
-    me = y * 32 + sp
-    at = lax.broadcasted_iota(jnp.int32, (CHIPS, LANES), 1)
-    table = jnp.full((CHIPS, LANES), -1, jnp.int32)
-    for core in range(2):
-        listed = lists[:, core, 0, :] + 1
-        hit = lists[:, core, 1, :] == me
-        first = jnp.min(jnp.where(hit, at, LANES), axis=1, keepdims=True)
-        last = jnp.max(jnp.where(hit, at, -1), axis=1, keepdims=True)
-        one = jnp.sum(jnp.where(at == first, listed, 0), axis=1, keepdims=True) - 1
-        two = jnp.sum(jnp.where((at == last) & (last > first), listed, 0), axis=1, keepdims=True) - 1
-        table = jnp.where(at == 2 * core, one, jnp.where(at == 2 * core + 1, two, table))
-    ids[...] = table
-
+
+    def first_list():
+        load_blk.wait()
+        load_own.wait()
+        list_step(0)
+
+    twist(0)
+    twist(1)
+
+    events = [(1.5, first_list, ())]
+    events += [(t, list_step, (n + 1,)) for n, t in enumerate((3.7, 7.7, 11.6, 16.6))]
+    events += [(CHOOSE_AT, choose_all, ())]
     for j in range(6):
-        ag1_finish(j)
-    for j in range(6):
-        ag2_finish(j)
-    for j in range(6):
-        ag3_finish(j)
-    for j in range(6):
-        ag4_finish(j)
+        steps = (dots, core_finish, rs1_finish, reduce_finish, ag1_finish, ag2_finish, ag3_finish, ag4_finish)
+        events += [(j + t, step, (j,)) for step, t in zip(steps, STAGE_AT)]
+    for _, step, args in sorted(events, key=lambda e: e[0]):
+        step(*args)
     for j in range(6):
         for n in range(7):
             sib_copy(j, n).wait_recv()
 
-    own_rows = rb // 4
-    out_rows = 4 * CAP * own_rows
-    in_rows = 4 * rb
-    rho = lax.broadcasted_iota(jnp.int32, (out_rows, in_rows), 0)
-    kappa = lax.broadcasted_iota(jnp.int32, (out_rows, in_rows), 1)
-    dev = rho // (CAP * own_rows)
-    target = dev * own_rows + rho // CAP % own_rows
-    which = dev * CAP + rho % CAP
-
-    def pick(n, carry):
+    def pick(n):
         gy_, g = n // 8, n % 8
         bands = []
         for u in range(2):
@@ -364,37 +377,35 @@
                 bands.append(
                     jnp.concatenate([every[u, j, chip_index(where, GATHER_AXES[j])] for j in range(6)], axis=1)
                 )
-        source = jnp.concatenate(bands, axis=0)
-        want = target
-        for half in range(2):
-            chip = chip_index((gy_, g // 2, g % 2 * 2 + half), LIST_AXES)
-            listed = ids[pl.ds(chip, 1), :]
-            for lane_ in range(4):
-                want = jnp.where(which == half * 4 + lane_, target + listed[:, lane_ : lane_ + 1] * rb, want)
-        chosen = (kappa == want).astype(F32).astype(BF)
-        rows[pl.ds(pl.multiple_of(n * out_rows, out_rows), out_rows), :] = jnp.dot(
-            chosen, source, preferred_element_type=F32
-        ).astype(BF)
+        return jnp.dot(chosen[n], jnp.concatenate(bands, axis=0), preferred_element_type=F32).astype(BF)
+
+    chunk = 4 * out_rows
+
+    def store(i):
+        at = pl.ds(pl.multiple_of(i * chunk, chunk), chunk)
+        return pltpu.make_async_copy(rows.at[at], picked.at[at], row_sem.at[i])
+
+    def pick_four(i, carry):
+        for n in range(4):
+            at = pl.ds(pl.multiple_of((i * 4 + n) * out_rows, out_rows), out_rows)
+            rows[at, :] = pick(i * 4 + n)
+        store(i).start()
         return carry
 
-    lax.fori_loop(0, CHIPS // 2, pick, 0)
-    store = pltpu.make_async_copy(rows, picked, row_sem)
-    store.start()
-
-    for h in range(2):
-        core_copy(h).wait_send()
+    lax.fori_loop(0, 8, pick_four, 0)
+
     for j in range(6):
+        core_copy(j).wait_send()
         for copy in rs1_copies(j) + rs2_copies(j) + ag1_copies(j) + ag2_copies(j):
             copy.wait_send()
         for g in range(4):
             for way in range(2):
                 ag3_copy(j, g, way).wait_send()
             fwd_copy(j, g).wait_send()
-        for g in range(4):
-            pass
         for n in range(7):
             sib_copy(j, n).wait_send()
-    store.wait()
+    for i in range(8):
+        store(i).wait()
 
 
 def product_kernel(rows, pair, out, kernel):
@@ -425,12 +436,12 @@
         out_specs=anywhere,
         scratch_shapes=[
             pltpu.VMEM((2, 2, colors, sites, width), BF),
-            pltpu.VMEM((colors, width, 2 * sites), BF),
-            pltpu.VMEM((colors, width, 2 * sites), BF),
-            pltpu.VMEM((colors, 2 * sites, 2 * width), BF),
+            pltpu.VMEM((2, width, 2 * colors * sites), BF),
+            pltpu.VMEM((2, width, 2 * colors * sites), BF),
+            pltpu.VMEM((2, 3, 2 * colors * sites, 2 * LANES), BF),
             pltpu.VMEM((sites, 8), F32),
-            pltpu.VMEM((2, PLANE, rb, width), BF),
-            pltpu.VMEM((2, PLANE, rb, width), BF),
+            pltpu.VMEM((6, PLANE, rb, LANES), BF),
+            pltpu.VMEM((6, PLANE, rb, LANES), BF),
             pltpu.VMEM((6, PLANE, rb, LANES), F32),
             pltpu.VMEM((6, PLANE, rb, LANES), BF),
             pltpu.VMEM((6, 3, 4, rb, LANES), BF),
@@ -438,19 +449,20 @@
             pltpu.VMEM((2, 6, CHIPS, rb, LANES), BF),
             pltpu.VMEM((CHIPS, 2, 2, LANES), jnp.int32),
             pltpu.VMEM((CHIPS, LANES), jnp.int32),
+            pltpu.VMEM((CHIPS // 2, 8 * own_rows, 4 * rb), BF),
             pltpu.VMEM((total, 2 * width), BF),
             pltpu.SemaphoreType.DMA((2 * colors + 2,)),
-            pltpu.SemaphoreType.DMA((2, 2)),
+            pltpu.SemaphoreType.DMA((2, 6)),
             pltpu.SemaphoreType.DMA((2, 4, 3)),
             pltpu.SemaphoreType.DMA((2, 6, 2, 3)),
             pltpu.SemaphoreType.DMA((2, 6, 2, 3)),
             pltpu.SemaphoreType.DMA((2, 6, 4, 2)),
             pltpu.SemaphoreType.DMA((2, 6, 4)),
             pltpu.SemaphoreType.DMA((2, 6, 7)),
-            pltpu.SemaphoreType.DMA,
+            pltpu.SemaphoreType.DMA((8,)),
         ],
         compiler_params=pltpu.CompilerParams(
-            collective_id=0, has_side_effects=True, vmem_limit_bytes=56 * 1024 * 1024
+            collective_id=0, has_side_effects=True, vmem_limit_bytes=60 * 1024 * 1024
         ),
         name="gather_elementals",
     )(momenta, vectors, item_block, item_owner)

time: 86 us -> 75.9 us (0.88)
  Pallas kernels: 85.7 us -> 75.6 us
    pallas_call x1, Pallas kernels: 76.3 us -> 66.2 us  [body(): pl.pallas_call(gather_kernel, out_shape=jax.ShapeDtypeStruct((total, 2 *...]
where the time goes in v4:
time: 75.9 us; the launch traced here: 75.6 us
  Pallas kernels  75.6 us (100%)
    pallas_call x1, Pallas kernels, body(): pl.pallas_call(gather_kernel, out_shape=jax.ShapeDtypeStruct((total, 2 *...  66.2 us
    pallas_call x1, Pallas kernels, body(): pl.pallas_call(product_kernel, out_shape=jax.ShapeDtypeStruct((total // 2...  9.43 us

profile of v4, /device:TPU:1, one launch (start us, length us, event | category | flops | bytes accessed | tf_op | source)
XLA Modules:
  0.0 75.6 jit_solution(10653158815752740058)
XLA Ops:
  0.0 66.2 %gather_elementals.1.rows = bf16[3072,768]{1,0:T(8,128)(2,1)} custom-call(s32[2,3]{1,0:T(2,128)} %mom.1, bf16[2,2,3,512,384]{4,3,2,1,0:T(8,128)(2,1)} %vec.1, s32[1,128]{1,0:T(1,128)} %blk_in.1, s32[1,128]{1,0:T(1,128)} %own_in.1), custom_call_target="tpu_custom_call" | custom-call | tf_op jit(solution)/shard_map/gather_elementals/pallas_call | solution.py:432
  66.2 9.4 %contract_perambulators.1 = bf16[1536,2,768]{2,1,0:T(2,128)(2,1)} custom-call(bf16[3072,768]{1,0:T(8,128)(2,1)} %gather_elementals.1.rows, bf16[2,384,384]{2,1,0:T(8,128)(2,1)} %bitcast.4), custom_call_target="tpu_custom_call" | custom-call | tf_op jit(solution)/shard_map/contract_perambulators/pallas_call | solution.py:470

commit v5 on v4

--- a/solution.py
+++ b/solution.py
@@ -19,10 +19,10 @@
 
 Y, X, Z = 0, 1, 2
 REDUCE_AXES = ((X, Z), (Z, X), (X, Z), (Z, X), (X, Z), (Z, X))
-GATHER_AXES = ((X, Z, Y), (Y, Z, X), (X, Z, Y), (X, Y, Z), (X, Z, Y), (Z, Y, X))
+GATHER_AXES = ((Y, X, Z), (X, Z, Y), (Z, Y, X), (Y, Z, X), (X, Y, Z), (Z, X, Y))
 LIST_AXES = (Z, X, Y)
-STAGE_AT = (0.0, 2.2, 5.6, 8.7, 12.2, 15.7, 20.7, 24.2)
-CHOOSE_AT = 21.3
+STAGE_AT = (0.0, 2.2, 5.6, 8.7, 12.7, 17.2, 22.7, 27.2)
+CHOOSE_AT = 17.9
 
 
 def plane_index(place, j):

time: 75.9 us -> 70.2 us (0.925)
  Pallas kernels: 75.6 us -> 69.9 us
    pallas_call x1, Pallas kernels: 66.2 us -> 60.5 us  [body(): pl.pallas_call(gather_kernel, out_shape=jax.ShapeDtypeStruct((total, 2 *...]
where the time goes in v5:
time: 70.2 us; the launch traced here: 69.9 us
  Pallas kernels  69.9 us (100%)
    pallas_call x1, Pallas kernels, body(): pl.pallas_call(gather_kernel, out_shape=jax.ShapeDtypeStruct((total, 2 *...  60.5 us
    pallas_call x1, Pallas kernels, body(): pl.pallas_call(product_kernel, out_shape=jax.ShapeDtypeStruct((total // 2...  9.43 us

profile of v5, /device:TPU:1, one launch (start us, length us, event | category | flops | bytes accessed | tf_op | source)
XLA Modules:
  0.0 69.9 jit_solution(1685173154370483600)
XLA Ops:
  0.0 60.5 %gather_elementals.1.rows = bf16[3072,768]{1,0:T(8,128)(2,1)} custom-call(s32[2,3]{1,0:T(2,128)} %mom.1, bf16[2,2,3,512,384]{4,3,2,1,0:T(8,128)(2,1)} %vec.1, s32[1,128]{1,0:T(1,128)} %blk_in.1, s32[1,128]{1,0:T(1,128)} %own_in.1), custom_call_target="tpu_custom_call" | custom-call | tf_op jit(solution)/shard_map/gather_elementals/pallas_call | solution.py:432
  60.5 9.4 %contract_perambulators.1 = bf16[1536,2,768]{2,1,0:T(2,128)(2,1)} custom-call(bf16[3072,768]{1,0:T(8,128)(2,1)} %gather_elementals.1.rows, bf16[2,384,384]{2,1,0:T(8,128)(2,1)} %bitcast.4), custom_call_target="tpu_custom_call" | custom-call | tf_op jit(solution)/shard_map/contract_perambulators/pallas_call | solution.py:470

commit v6 on v5

--- a/solution.py
+++ b/solution.py
@@ -466,7 +466,7 @@
         ),
         name="gather_elementals",
     )(momenta, vectors, item_block, item_owner)
-    tile = 384
+    tile = 768
     out = pl.pallas_call(
         product_kernel,
         out_shape=jax.ShapeDtypeStruct((total // 2, 2, 2 * width), BF),

time: 70.2 us -> 68.4 us (0.974)
  Pallas kernels: 69.9 us -> 68.2 us
    pallas_call x1, Pallas kernels: 9.43 us -> 7.72 us  [body(): pl.pallas_call(product_kernel, out_shape=jax.ShapeDtypeStruct((total // 2...]
where the time goes in v6:
time: 68.4 us; the launch traced here: 68.2 us
  Pallas kernels  68.2 us (100%)
    pallas_call x1, Pallas kernels, body(): pl.pallas_call(gather_kernel, out_shape=jax.ShapeDtypeStruct((total, 2 *...  60.5 us
    pallas_call x1, Pallas kernels, body(): pl.pallas_call(product_kernel, out_shape=jax.ShapeDtypeStruct((total // 2...  7.72 us

profile of v6, /device:TPU:1, one launch (start us, length us, event | category | flops | bytes accessed | tf_op | source)
XLA Modules:
  0.0 68.2 jit_solution(3663745320335304875)
XLA Ops:
  0.0 60.5 %gather_elementals.1.rows = bf16[3072,768]{1,0:T(8,128)(2,1)} custom-call(s32[2,3]{1,0:T(2,128)} %mom.1, bf16[2,2,3,512,384]{4,3,2,1,0:T(8,128)(2,1)} %vec.1, s32[1,128]{1,0:T(1,128)} %blk_in.1, s32[1,128]{1,0:T(1,128)} %own_in.1), custom_call_target="tpu_custom_call" | custom-call | tf_op jit(solution)/shard_map/gather_elementals/pallas_call | solution.py:432
  60.5 7.7 %contract_perambulators.1 = bf16[1536,2,768]{2,1,0:T(2,128)(2,1)} custom-call(bf16[3072,768]{1,0:T(8,128)(2,1)} %gather_elementals.1.rows, bf16[2,384,384]{2,1,0:T(8,128)(2,1)} %bitcast.4), custom_call_target="tpu_custom_call" | custom-call | tf_op jit(solution)/shard_map/contract_perambulators/pallas_call | solution.py:470

commit v7 on v6

--- a/solution.py
+++ b/solution.py
@@ -379,20 +379,20 @@
                 )
         return jnp.dot(chosen[n], jnp.concatenate(bands, axis=0), preferred_element_type=F32).astype(BF)
 
-    chunk = 4 * out_rows
+    chunk = 8 * out_rows
 
     def store(i):
         at = pl.ds(pl.multiple_of(i * chunk, chunk), chunk)
         return pltpu.make_async_copy(rows.at[at], picked.at[at], row_sem.at[i])
 
-    def pick_four(i, carry):
-        for n in range(4):
-            at = pl.ds(pl.multiple_of((i * 4 + n) * out_rows, out_rows), out_rows)
-            rows[at, :] = pick(i * 4 + n)
+    def pick_eight(i, carry):
+        for n in range(8):
+            at = pl.ds(pl.multiple_of((i * 8 + n) * out_rows, out_rows), out_rows)
+            rows[at, :] = pick(i * 8 + n)
         store(i).start()
         return carry
 
-    lax.fori_loop(0, 8, pick_four, 0)
+    lax.fori_loop(0, 4, pick_eight, 0)
 
     for j in range(6):
         core_copy(j).wait_send()
@@ -404,7 +404,7 @@
             fwd_copy(j, g).wait_send()
         for n in range(7):
             sib_copy(j, n).wait_send()
-    for i in range(8):
+    for i in range(4):
         store(i).wait()
 
 
@@ -459,7 +459,7 @@
             pltpu.SemaphoreType.DMA((2, 6, 4, 2)),
             pltpu.SemaphoreType.DMA((2, 6, 4)),
             pltpu.SemaphoreType.DMA((2, 6, 7)),
-            pltpu.SemaphoreType.DMA((8,)),
+            pltpu.SemaphoreType.DMA((4,)),
         ],
         compiler_params=pltpu.CompilerParams(
             collective_id=0, has_side_effects=True, vmem_limit_bytes=60 * 1024 * 1024

time: 68.4 us -> 67.9 us (level)
  no operation moved by 1% of the time
where the time goes in v7:
time: 67.9 us; the launch traced here: 67.7 us
  Pallas kernels  67.7 us (100%)
    pallas_call x1, Pallas kernels, body(): pl.pallas_call(gather_kernel, out_shape=jax.ShapeDtypeStruct((total, 2 *...  60 us
    pallas_call x1, Pallas kernels, body(): pl.pallas_call(product_kernel, out_shape=jax.ShapeDtypeStruct((total // 2...  7.72 us

profile of v7, /device:TPU:1, one launch (start us, length us, event | category | flops | bytes accessed | tf_op | source)
XLA Modules:
  0.0 67.7 jit_solution(4300883855261021788)
XLA Ops:
  0.0 60.0 %gather_elementals.1.rows = bf16[3072,768]{1,0:T(8,128)(2,1)} custom-call(s32[2,3]{1,0:T(2,128)} %mom.1, bf16[2,2,3,512,384]{4,3,2,1,0:T(8,128)(2,1)} %vec.1, s32[1,128]{1,0:T(1,128)} %blk_in.1, s32[1,128]{1,0:T(1,128)} %own_in.1), custom_call_target="tpu_custom_call" | custom-call | tf_op jit(solution)/shard_map/gather_elementals/pallas_call | solution.py:432
  60.0 7.7 %contract_perambulators.1 = bf16[1536,2,768]{2,1,0:T(2,128)(2,1)} custom-call(bf16[3072,768]{1,0:T(8,128)(2,1)} %gather_elementals.1.rows, bf16[2,384,384]{2,1,0:T(8,128)(2,1)} %bitcast.4), custom_call_target="tpu_custom_call" | custom-call | tf_op jit(solution)/shard_map/contract_perambulators/pallas_call | solution.py:470
